TPU v7x, 512 devices: a whole 4x4x16 slice. The times are simulated.
512 devices in a mesh: wide: 32 (over z_hi, x, core), blk: 16 (over z_lo, y).
Axes of the slice: x: 4, y: 4, z: 16 (z_hi: 4, z_lo: 4; z = z_hi * 4 + z_lo), core: 2. Of those that a mesh axis runs over, the one named last changes fastest.
Arguments:
- sources: bfloat16 [512, 64000], P(('wide', 'blk')), may hold values from -6 to 6
- targets: bfloat16 [16, 64000], P('blk'), may hold values from -6 to 6
Outputs:
- exchange_field: float32 [16, 64000], P('blk', 'wide')
All inputs are finite; a program needn't handle non-finite values.
Results may differ from a plain program's by a relative error of at most 0.014.
Values may be sent and summed in bfloat16 or wider, within the bound.
No kernel may reach another device: no remote copies, remote signals or barrier semaphores. Data moves between devices by JAX's collectives and lax.ppermute only.
A program may use at most 64 MiB of HBM per device.

v0:
```python
import math

import jax
import jax.numpy as jnp
from jax import lax
from jax.sharding import PartitionSpec as P

GRID = 40
HOPS = 2


screen = 0.3


def from_behind(block, axis, distance):
    devices = range(lax.axis_size(axis))
    route = [((i - distance) % len(devices), i) for i in devices]
    return lax.ppermute(block, axis, route)


def in_blocks(array, dim, count):
    dims = array.shape
    parts = array.reshape(*dims[:dim], count, dims[dim] // count, *dims[dim + 1 :])
    return jnp.moveaxis(parts, dim, 0)


def sent_and_summed(array, axis, dim):
    parts = in_blocks(array, dim, lax.axis_size(axis))
    arrived = lax.all_to_all(parts, axis, split_axis=0, concat_axis=0, tiled=True)
    return arrived.astype(jnp.float32).sum(axis=0)


def tables(grid):
    index = jnp.arange(grid, dtype=jnp.int32)
    product = index[:, None] * index[None, :] % grid
    angle = 2.0 * math.pi / grid * product.astype(jnp.float32)
    return jnp.concatenate([jnp.cos(angle), jnp.sin(angle)], axis=0).astype(jnp.bfloat16)


def kernel_table(grid):
    index = jnp.arange(grid, dtype=jnp.int32)
    wrapped = (index + grid // 2) % grid - grid // 2
    wave = 2.0 * math.pi / grid * wrapped.astype(jnp.float32)
    square = wave * wave
    total = square[:, None, None] + square[None, :, None] + square[None, None, :]
    values = 4.0 * math.pi / (total + screen * screen) / float(grid**3)
    return values.reshape(grid, grid * grid)


def turn(field, both):
    width = both.shape[1]
    cos_table = both[:width]
    sin_table = both[width:]
    cpart = jnp.einsum("mnr,kn->mrk", field, cos_table, preferred_element_type=jnp.float32)
    spart = jnp.einsum("mnr,kn->mrk", field, sin_table, preferred_element_type=jnp.float32)
    return (cpart.reshape(field.shape), spart.reshape(field.shape))


def potential(pair, both, kern):
    cpart, spart = turn(pair, both)
    real_part = cpart.astype(jnp.bfloat16)
    imag_part = (-spart).astype(jnp.bfloat16)
    for section in range(2):
        rcos, rsin = turn(real_part, both)
        icos, isin = turn(imag_part, both)
        new_real = rcos + isin
        new_imag = icos - rsin
        if section == 1:
            new_real = new_real * kern
            new_imag = new_imag * kern
        real_part = new_real.astype(jnp.bfloat16)
        imag_part = new_imag.astype(jnp.bfloat16)
    for section in range(2):
        rcos, rsin = turn(real_part, both)
        icos, isin = turn(imag_part, both)
        real_part = (rcos - isin).astype(jnp.bfloat16)
        imag_part = (icos + rsin).astype(jnp.bfloat16)
    rcos, rsin = turn(real_part, both)
    icos, isin = turn(imag_part, both)
    return rcos - isin


def exchange_term(chosen, target, both, kern):
    grid = both.shape[1]
    count = chosen.shape[0]
    pair = (chosen.astype(jnp.float32) * target.astype(jnp.float32)).astype(jnp.bfloat16)
    pair = pair.reshape(count, grid, grid * grid)
    field = potential(pair, both, kern).reshape(count, grid**3)
    return -jnp.sum(chosen.astype(jnp.float32) * field, axis=0, keepdims=True)


def shards(sources, targets):
    both = tables(GRID)
    kern = kernel_table(GRID)
    partial_value = None
    for step in range(HOPS):
        if step == 0:
            nearby = sources
        else:
            nearby = from_behind(sources, "blk", -step)
        term = exchange_term(nearby, targets, both, kern)
        partial_value = term if partial_value is None else partial_value + term
    summed = sent_and_summed(partial_value.astype(jnp.bfloat16), "wide", 1)
    summed = from_behind(summed, "blk", HOPS - 1)
    return summed


def solution(mesh):
    in_specs = (P(("wide", "blk"), None), P("blk", None))
    out_specs = P("blk", "wide")
    return jax.shard_map(shards, mesh=mesh, in_specs=in_specs, out_specs=out_specs, check_vma=False)
```

profile of v0, /device:TPU:1, one launch (start us, length us, event | category | flops | bytes accessed | tf_op | source)
XLA Modules:
  0.0 85.8 jit_solution(9974737262620754537)
XLA Ops:
  0.0 9.5 %collective-permute-start = (bf16[1,64000]{1,0:T(2,128)(2,1)}, bf16[1,64000]{1,0:T(2,128)(2,1)S(1)}, u32[]{:S(2)}, u32[]{:S(2)}) collective-permute-start(bf16[1,64000]{1,0:T(2,128)(2,1)} %param.2), channel_id=1, source_target_pairs={{1,0},{2,1},{3,2},{4,3},{5,4},{6,5},{7,6},{8,7},{9,8},{10,9},{11,1... | collective-permute-start | bytes 384008 | tf_op jit(solution)/shard_map/ppermute | solution.py:18
  10.3 4.4 %collective-permute-done = bf16[1,64000]{1,0:T(2,128)(2,1)S(1)} collective-permute-done((bf16[1,64000]{1,0:T(2,128)(2,1)}, bf16[1,64000]{1,0:T(2,128)(2,1)S(1)}, u32[]{:S(2)}, u32[]{:S(2)}) %collective-permute-start) | collective-permute-done | bytes 128032 | tf_op jit(solution)/shard_map/ppermute | solution.py:18
  14.7 2.0 %convert_reduce_fusion.3 = (bf16[64000]{0:T(1024)(128)(2,1)S(1)}, bf16[64000]{0:T(1024)(128)(2,1)S(1)}) fusion(bf16[1,64000]{1,0:T(2,128)(2,1)S(1)} %copy-done.1, bf16[1,64000]{1,0:T(2,128)(2,1)S(1)} %copy-done, bf16[1,64000]{1,0:T(2,128)(2,1)S(1)} %collective-permute-done), kind=kLoop, calls=%fused_computation.44 | loop fusion | flops 448000 | bytes 640000 | tf_op jit(solution)/shard_map/convert_element_type | solution.py:86
  18.3 0.3 convert_element_type.339
  20.2 0.3 convert_element_type.343
  21.2 0.3 convert_element_type.345
  22.0 0.3 copy.40
  22.9 0.3 copy.41
  23.7 0.3 convert_element_type.318
  24.5 0.3 convert_element_type.320
  25.5 0.3 convert_element_type.322
  26.6 0.3 convert_element_type.324
  27.4 0.3 copy.29
  28.2 0.3 copy.30
  29.9 0.5 convert_element_type.331
  31.2 0.3 convert_element_type.329
  32.2 0.3 convert_element_type.335
  33.0 0.3 convert_element_type.333
  33.8 0.3 copy.35
  34.1 0.7 sub.112
  35.9 0.3 convert_element_type.351
  37.0 0.3 convert_element_type.349
  38.8 0.3 convert_element_type.353
  39.6 0.3 copy.46
  39.9 0.7 sub.119
  40.6 1.2 %convert_reduce_fusion.1 = bf16[64000]{0:T(1024)(128)(2,1)S(1)} fusion(f32[1,64000]{1,0:T(1,128)S(1)} %sub.119, bf16[1,64000]{1,0:T(2,128)(2,1)S(1)} %collective-permute-done, f32[1,64000]{1,0:T(1,128)S(1)} %sub.112, bf16[1,64000]{1,0:T(2,128)(2,1)S(1)} %copy-done), kind=kLoop, calls=%fused_computation.42 | loop fusion | flops 512000 | bytes 896000 | tf_op jit(solution)/shard_map/convert_element_type | solution.py:103
  42.0 0.5 broadcast.220
  42.5 1.4 %reduce.7 = bf16[32,2000]{1,0:T(8,128)(2,1)S(1)} reduce(bf16[32,1,2000]{2,1,0:T(2,128)(2,1)S(1)} %transpose_reshape.4, bf16[]{:T(256)} %broadcast.220), dimensions={1}, to_apply=%transpose_reshape.4.reduce_sub_computation | reduce | bytes 256002 | tf_op jit(solution)/shard_map/transpose;reshape | solution.py:24
  44.1 32.4 %all_to_all.5 = bf16[32,2,1000]{2,1,0:T(2,128)(2,1)S(1)} all-to-all(bf16[32,2,1000]{2,1,0:T(2,128)(2,1)S(1)} %reshape.612), channel_id=1, replica_groups=mesh['wide'=32,'blk'=16] {'wide'}, dimensions={0} | all-to-all | bytes 256000 | tf_op jit(solution)/shard_map/all_to_all | solution.py:29
  76.9 2.1 %collective-permute-start.1 = (f32[1,2000]{1,0:T(1,128)S(1)}, f32[1,2000]{1,0:T(1,128)S(1)}, u32[]{:S(2)}, u32[]{:S(2)}) collective-permute-start(f32[1,2000]{1,0:T(1,128)S(1)} %bitcast.41), channel_id=1, source_target_pairs={{15,0},{0,1},{1,2},{2,3},{3,4},{4,5},{5,6},{6,7},{7,8},{8,9},{9,10... | collective-permute-start | bytes 24008 | tf_op jit(solution)/shard_map/ppermute | solution.py:18
  79.1 6.2 %collective-permute-done.1 = f32[1,2000]{1,0:T(1,128)S(1)} collective-permute-done((f32[1,2000]{1,0:T(1,128)S(1)}, f32[1,2000]{1,0:T(1,128)S(1)}, u32[]{:S(2)}, u32[]{:S(2)}) %collective-permute-start.1) | collective-permute-done | bytes 8032 | tf_op jit(solution)/shard_map/ppermute | solution.py:18
  85.2 0.6 copy.49
  (79 shorter events, 17.7 us)
Async XLA Ops:
  0.0 14.7 %collective-permute-start = (bf16[1,64000]{1,0:T(2,128)(2,1)}, bf16[1,64000]{1,0:T(2,128)(2,1)S(1)}, u32[]{:S(2)}, u32[]{:S(2)}) collective-permute-start(bf16[1,64000]{1,0:T(2,128)(2,1)} %param.2), channel_id=1, source_target_pairs={{1,0},{2,1},{3,2},{4,3},{5,4},{6,5},{7,6},{8,7},{9,8},{10,9},{11,1... | collective-permute-start | bytes 384008 | tf_op jit(solution)/shard_map/ppermute | solution.py:18
  9.9 4.8 %copy-start = (bf16[1,64000]{1,0:T(2,128)(2,1)S(1)}, bf16[1,64000]{1,0:T(2,128)(2,1)}, u32[]{:S(2)}) copy-start(bf16[1,64000]{1,0:T(2,128)(2,1)} %param.2) | copy-start | bytes 384004
  9.9 4.8 %copy-start.1 = (bf16[1,64000]{1,0:T(2,128)(2,1)S(1)}, bf16[1,64000]{1,0:T(2,128)(2,1)}, u32[]{:S(2)}) copy-start(bf16[1,64000]{1,0:T(2,128)(2,1)} %param.3) | copy-start | bytes 384004
  76.9 8.3 %collective-permute-start.1 = (f32[1,2000]{1,0:T(1,128)S(1)}, f32[1,2000]{1,0:T(1,128)S(1)}, u32[]{:S(2)}, u32[]{:S(2)}) collective-permute-start(f32[1,2000]{1,0:T(1,128)S(1)} %bitcast.41), channel_id=1, source_target_pairs={{15,0},{0,1},{1,2},{2,3},{3,4},{4,5},{5,6},{6,7},{7,8},{8,9},{9,10... | collective-permute-start | bytes 24008 | tf_op jit(solution)/shard_map/ppermute | solution.py:18
where the time goes:
time: 86 us; the launch traced here: 85.8 us
  blocking collectives  32.4 us (38%)
  local copies, waits for them, and re-layouts  15.4 us (18%)
  starting transfers between devices  11.6 us (13%)
  waiting for transfers between devices  10.6 us (12%)
  matrix products  10.2 us (12%)
  other arithmetic  5.11 us (6%)
    all_to_all x1, blocking collectives, sent_and_summed(): lax.all_to_all(parts, axis, split_axis=0, concat_axis=0, tiled=True)  32.4 us
    ppermute x2, starting transfers between devices, from_behind(): return lax.ppermute(block, axis, route)  11.6 us
    ppermute x2, waiting for transfers between devices, from_behind(): return lax.ppermute(block, axis, route)  10.6 us
    dot_general x20, matrix products, turn(): jnp.einsum('mnr,kn->mrk', field, sin_table, preferred_element_type=jnp.fl...  5.18 us
    dot_general x20, matrix products, turn(): jnp.einsum('mnr,kn->mrk', field, cos_table, preferred_element_type=jnp.fl...  4.97 us
    convert_element_type x8, local copies, waits for them, and re-layouts, potential(): imag_part = (icos + rsin).astype(jnp.bfloat16)  2.28 us
    convert_element_type x8, local copies, waits for them, and re-layouts, potential(): real_part = (rcos - isin).astype(jnp.bfloat16)  2.1 us
    convert_element_type x1, other arithmetic, exchange_term(): (chosen.astype(jnp.float32) * target.astype(jnp.float32)).astype(jnp.bflo...  2.02 us
  transfers between devices with their start and end apart: 2, of which 2 were waited for; matrix products, arithmetic and copies ran while one was open for 1% of the time, Pallas kernels for 0%

commit v1 on v0

v1 whole, which is shorter than its diff:
```python
import functools
import math

import jax
import jax.numpy as jnp
import numpy as np
from jax import lax
from jax.experimental import pallas as pl
from jax.experimental.pallas import tpu as pltpu
from jax.sharding import PartitionSpec as P

GRID = 40
ROWS = GRID * GRID
LANES = 128
HALF = 64
PIECES = 32
PIECE = GRID**3 // PIECES
GROUPS = PIECE // GRID
SCREEN = 0.3


def tables():
    index = np.arange(GRID)
    product = index[:, None] * index[None, :] % GRID
    folded = np.minimum(product, GRID - product)
    angle = 2.0 * math.pi / GRID * folded
    cos = np.cos(angle)
    sin = np.where(product <= GRID // 2, 1.0, -1.0) * np.sin(angle)
    sin = np.where((product == 0) | (product == GRID // 2), 0.0, sin)
    return cos.astype(np.float32), sin.astype(np.float32)


def weights():
    cos, sin = tables()
    left = np.concatenate([cos, sin], axis=1)

    def right(sign):
        out = np.zeros((LANES, LANES), np.float32)
        out[:GRID, :GRID] = cos
        out[:GRID, HALF : HALF + GRID] = -sign * sin
        out[HALF : HALF + GRID, :GRID] = sign * sin
        out[HALF : HALF + GRID, HALF : HALF + GRID] = cos
        return out

    return left, right(1.0), right(-1.0)


def kernel_table():
    index = jnp.arange(GRID, dtype=jnp.int32)
    wrapped = (index + GRID // 2) % GRID - GRID // 2
    wave = 2.0 * math.pi / GRID * wrapped.astype(jnp.float32)
    square = wave * wave
    lane = jnp.arange(LANES, dtype=jnp.int32) % HALF
    lane_wrapped = (lane + GRID // 2) % GRID - GRID // 2
    lane_wave = 2.0 * math.pi / GRID * lane_wrapped.astype(jnp.float32)
    lane_square = lane_wave * lane_wave
    total = square[None, :, None] + square[:, None, None] + lane_square[None, None, :]
    return 4.0 * math.pi / (total + SCREEN * SCREEN) / float(GRID**3)


def body(s0_ref, s1_ref, t_ref, kern_ref, left_ref, fwd_ref, inv_ref, out_ref, xs, flat):
    lane = lax.broadcasted_iota(jnp.int32, (PIECES, LANES), 1)
    low = lane < HALF
    wide = flat.shape[2]

    target = t_ref[...].astype(jnp.float32)
    flat[0, :, :PIECE] = s0_ref[...].astype(jnp.float32) * target
    flat[1, :, :PIECE] = s1_ref[...].astype(jnp.float32) * target
    flat[:, :, PIECE:] = jnp.zeros((2, PIECES, wide - PIECE), jnp.float32)

    def aligned(which, group, to):
        start = GRID * group
        tile, shift = start // LANES, start % LANES
        value = flat[which, :, tile * LANES : (tile + 1) * LANES]
        if shift + GRID > LANES:
            after = flat[which, :, (tile + 1) * LANES : (tile + 2) * LANES]
            value = jnp.where(lane >= shift, value, after)
        turn = (to - shift) % LANES
        return pltpu.roll(value, turn, 1) if turn else value

    for group in range(GROUPS):
        merged = jnp.where(low, aligned(0, group, 0), aligned(1, group, HALF))
        xs[pl.ds(group, PIECES, stride=GROUPS), :] = merged

    left = left_ref[...]
    slab_lane = lax.broadcasted_iota(jnp.int32, (GRID, LANES), 1)
    forward_sign = jnp.where(slab_lane < HALF, 1.0, -1.0).astype(jnp.float32)

    def stacked(slab, sign):
        return jnp.concatenate([slab, pltpu.roll(slab, HALF, 1) * sign], axis=0)

    def left_turn(first, second, sign):
        both = jnp.concatenate([stacked(first, sign), stacked(second, sign)], axis=1)
        return jnp.dot(left, both.astype(jnp.bfloat16), preferred_element_type=jnp.float32)

    def along_b(sign):
        for pair in range(GRID // 2):
            one, two = pl.ds(2 * pair * GRID, GRID), pl.ds((2 * pair + 1) * GRID, GRID)
            turned = left_turn(xs[one, :], xs[two, :], sign)
            xs[one, :] = turned[:, :LANES]
            xs[two, :] = turned[:, LANES:]

    xs[...] = jnp.dot(xs[...].astype(jnp.bfloat16), fwd_ref[...], preferred_element_type=jnp.float32)
    along_b(forward_sign)
    for pair in range(GRID // 2):
        one, two = pl.ds(2 * pair, GRID, stride=GRID), pl.ds(2 * pair + 1, GRID, stride=GRID)
        turned = left_turn(xs[one, :], xs[two, :], forward_sign)
        first = turned[:, :LANES] * kern_ref[2 * pair]
        second = turned[:, LANES:] * kern_ref[2 * pair + 1]
        turned = left_turn(first, second, -forward_sign)
        xs[one, :] = turned[:, :LANES]
        xs[two, :] = turned[:, LANES:]
    along_b(-forward_sign)
    xs[...] = jnp.dot(xs[...].astype(jnp.bfloat16), inv_ref[...], preferred_element_type=jnp.float32)

    tiles = [[None] * (wide // LANES) for _ in range(2)]
    for group in range(GROUPS):
        start = GRID * group
        tile, shift = start // LANES, start % LANES
        value = xs[pl.ds(group, PIECES, stride=GROUPS), :]
        for which in range(2):
            turn = (shift - HALF * which) % LANES
            moved = pltpu.roll(value, turn, 1) if turn else value
            held = tiles[which][tile]
            tiles[which][tile] = moved if held is None else jnp.where(lane >= shift, moved, held)
            if shift + GRID > LANES:
                tiles[which][tile + 1] = moved
    for tile in range(wide // LANES):
        size = min(LANES, PIECE - tile * LANES)
        here = slice(tile * LANES, tile * LANES + size)
        total = s0_ref[:, here].astype(jnp.float32) * tiles[0][tile][:, :size]
        total += s1_ref[:, here].astype(jnp.float32) * tiles[1][tile][:, :size]
        out_ref[:, here] = (-total).astype(jnp.bfloat16)


def exchange_term(s0, s1, target):
    left, fwd, inv = (jnp.asarray(w, jnp.bfloat16) for w in weights())
    wide = -(-PIECE // LANES) * LANES
    vmem = pl.BlockSpec(memory_space=pltpu.VMEM)
    return pl.pallas_call(
        body,
        out_shape=jax.ShapeDtypeStruct((PIECES, PIECE), jnp.bfloat16),
        in_specs=[vmem] * 7,
        out_specs=vmem,
        scratch_shapes=[
            pltpu.VMEM((ROWS, LANES), jnp.float32),
            pltpu.VMEM((2, PIECES, wide), jnp.float32),
        ],
        cost_estimate=pl.CostEstimate(flops=200_000_000, bytes_accessed=2_000_000, transcendentals=0),
        name="exchange",
    )(s0, s1, target, kernel_table(), left, fwd, inv)


def from_behind(block):
    count = lax.axis_size("blk")
    return lax.ppermute(block, "blk", [((i - 1) % count, i) for i in range(count)])


def shards(sources, targets):
    own = sources.reshape(PIECES, PIECE)
    target = from_behind(targets.reshape(PIECES, PIECE))
    behind = from_behind(own)
    partial = exchange_term(own, behind, target)
    arrived = lax.all_to_all(partial, "wide", split_axis=0, concat_axis=0, tiled=True)
    return arrived.astype(jnp.float32).sum(axis=0, keepdims=True)


def solution(mesh):
    in_specs = (P(("wide", "blk"), None), P("blk", None))
    return jax.shard_map(shards, mesh=mesh, in_specs=in_specs, out_specs=P("blk", "wide"), check_vma=False)
```

time: 86 us -> 60.2 us (0.70)
  local copies, waits for them, and re-layouts: 15.4 us -> 1.94 us
  matrix products: 10.2 us -> 0 us
  waiting for transfers between devices: 10.6 us -> 5.27 us
  Pallas kernels: 0 us -> 4.43 us
  starting transfers between devices: 11.6 us -> 7.23 us
  blocking collectives: 32.4 us -> 34.9 us
  other arithmetic: 5.11 us -> 6.15 us
    dot_general x40 -> x0, matrix products: 10.2 us -> none  [the longest x20 5.18 us: turn(): jnp.einsum('mnr,kn->mrk', field, sin_table, preferred_element_type=jnp.fl...]
    convert_element_type x32 -> x0, local copies, waits for them, and re-layouts: 8.59 us -> none  [the longest x8 2.28 us: potential(): imag_part = (icos + rsin).astype(jnp.bfloat16)]
    ppermute x2, waiting for transfers between devices: 10.6 us -> 5.27 us  [from_behind(): lax.ppermute(block, 'blk', [((i - 1) % count, i) for i in range(count)])]
    pallas_call x0 -> x1, Pallas kernels: none -> 4.43 us  [exchange_term(): pl.pallas_call(body, out_shape=jax.ShapeDtypeStruct((PIECES, PIECE), jnp....]
    ppermute x2, starting transfers between devices: 11.6 us -> 7.23 us  [from_behind(): lax.ppermute(block, 'blk', [((i - 1) % count, i) for i in range(count)])]
    convert_element_type x3 -> x0, other arithmetic: 3.37 us -> none  [the longest x1 2.02 us: exchange_term(): (chosen.astype(jnp.float32) * target.astype(jnp.float32)).astype(jnp.bflo...]
    sub x8 -> x0, local copies, waits for them, and re-layouts: 3.12 us -> none  [the longest x4 2.02 us: potential(): return rcos - isin]
    all_to_all x1, blocking collectives: 32.4 us -> 34.9 us  [shards(): lax.all_to_all(partial, 'wide', split_axis=0, concat_axis=0, tiled=True)]
  transfers between devices with their start and end apart: 2 -> 2, of which waited for: 2 -> 2; matrix products, arithmetic and copies ran while one was open for 1% -> 4% of each run, Pallas kernels for 0% -> 0%
where the time goes in v1:
time: 60.2 us; the launch traced here: 60 us
  blocking collectives  34.9 us (58%)
  starting transfers between devices  7.23 us (12%)
  other arithmetic  6.15 us (10%)
  waiting for transfers between devices  5.27 us (9%)
  Pallas kernels  4.43 us (7%)
  local copies, waits for them, and re-layouts  1.94 us (3%)
    all_to_all x1, blocking collectives, shards(): lax.all_to_all(partial, 'wide', split_axis=0, concat_axis=0, tiled=True)  34.9 us
    ppermute x2, starting transfers between devices, from_behind(): lax.ppermute(block, 'blk', [((i - 1) % count, i) for i in range(count)])  7.23 us
    ppermute x2, waiting for transfers between devices, from_behind(): lax.ppermute(block, 'blk', [((i - 1) % count, i) for i in range(count)])  5.27 us
    pallas_call x1, Pallas kernels, exchange_term(): pl.pallas_call(body, out_shape=jax.ShapeDtypeStruct((PIECES, PIECE), jnp....  4.43 us
    unnamed x2, other arithmetic  2.45 us
    all_to_all x1, other arithmetic, shards(): lax.all_to_all(partial, 'wide', split_axis=0, concat_axis=0, tiled=True)  1.58 us
  transfers between devices with their start and end apart: 2, of which 2 were waited for; matrix products, arithmetic and copies ran while one was open for 4% of the time, Pallas kernels for 0%

profile of v1, /device:TPU:1, one launch (start us, length us, event | category | flops | bytes accessed | tf_op | source)
XLA Modules:
  0.0 60.0 jit_solution(16791586310992313453)
XLA Ops:
  0.0 0.0 copy-start.1
  0.0 1.7 %reduce.1 = bf16[64000]{0:T(1024)(128)(2,1)S(1)} reduce(bf16[1,64000]{1,0:T(2,128)(2,1)} %param.5, bf16[]{:T(256)} %constant.59), dimensions={0}, to_apply=%param.5.reduce_sub_computation | reduce | bytes 256002 | tf_op args[0]
  1.7 0.2 reshape.89.s0_ref
  1.9 0.0 copy-start
  1.9 4.0 %collective-permute-start = (bf16[32,2000]{1,0:T(8,128)(2,1)S(1)}, bf16[32,2000]{1,0:T(8,128)(2,1)S(1)}, u32[]{:S(2)}, u32[]{:S(2)}) collective-permute-start(bf16[32,2000]{1,0:T(8,128)(2,1)S(1)} %reshape.89.s0_ref), channel_id=1, source_target_pairs={{15,0},{0,1},{1,2},{2,3},{3,4},{4,5},{5,6},{6,7},{7,8},{8,9},{9,10... | collective-permute-start | bytes 384008 | tf_op jit(solution)/shard_map/ppermute | solution.py:156
  6.0 0.0 copy-done.1
  6.0 0.7 %reduce.2 = bf16[64000]{0:T(1024)(128)(2,1)S(1)} reduce(bf16[1,64000]{1,0:T(2,128)(2,1)S(1)} %copy-done.1, bf16[]{:T(256)} %constant.59), dimensions={0}, to_apply=%param.6.reduce_sub_computation | reduce | bytes 256002 | tf_op args[1]
  6.7 0.0 copy-done
  6.7 0.2 reshape.90
  7.0 3.2 %collective-permute-start.1 = (bf16[32,2000]{1,0:T(8,128)(2,1)S(1)}, bf16[32,2000]{1,0:T(8,128)(2,1)S(1)}, u32[]{:S(2)}, u32[]{:S(2)}) collective-permute-start(bf16[32,2000]{1,0:T(8,128)(2,1)S(1)} %reshape.90), channel_id=1, source_target_pairs={{15,0},{0,1},{1,2},{2,3},{3,4},{4,5},{5,6},{6,7},{7,8},{8,9},{9,10... | collective-permute-start | bytes 384008 | tf_op jit(solution)/shard_map/ppermute | solution.py:156
  10.2 0.1 broadcast_add_fusion
  10.3 1.2 %divide_multiply_fusion.kern_ref = f32[40,40,128]{2,1,0:T(8,128)} fusion(f32[128]{0:T(128)S(1)} %fusion.9, f32[40,40]{1,0:T(8,128)S(1)} %broadcast_add_fusion), kind=kLoop, calls=%fused_computation | loop fusion | flops 819200 | bytes 826112 | tf_op jit(solution)/shard_map/div | solution.py:58
  11.5 2.3 %collective-permute-done.s1_ref = bf16[32,2000]{1,0:T(8,128)(2,1)S(1)} collective-permute-done((bf16[32,2000]{1,0:T(8,128)(2,1)S(1)}, bf16[32,2000]{1,0:T(8,128)(2,1)S(1)}, u32[]{:S(2)}, u32[]{:S(2)}) %collective-permute-start) | collective-permute-done | bytes 128032 | tf_op jit(solution)/shard_map/ppermute | solution.py:156
  13.8 0.0 copy-start.2
  13.8 2.9 %collective-permute-done.1.t_ref = bf16[32,2000]{1,0:T(8,128)(2,1)S(1)} collective-permute-done((bf16[32,2000]{1,0:T(8,128)(2,1)S(1)}, bf16[32,2000]{1,0:T(8,128)(2,1)S(1)}, u32[]{:S(2)}, u32[]{:S(2)}) %collective-permute-start.1) | collective-permute-done | bytes 128032 | tf_op jit(solution)/shard_map/ppermute | solution.py:156
  16.7 0.0 copy-done.2
  16.7 0.0 copy-start.3
  16.7 0.6 %copy-done.3 = bf16[32,2000]{1,0:T(8,128)(2,1)} copy-done((bf16[32,2000]{1,0:T(8,128)(2,1)}, bf16[32,2000]{1,0:T(8,128)(2,1)S(1)}, u32[]{:S(2)}) %copy-start.3) | copy-done | bytes 128024
  17.4 4.4 %exchange.1 = bf16[32,2000]{1,0:T(8,128)(2,1)} custom-call(bf16[32,2000]{1,0:T(8,128)(2,1)} %copy-done, bf16[32,2000]{1,0:T(8,128)(2,1)} %copy-done.2, bf16[32,2000]{1,0:T(8,128)(2,1)} %copy-done.3, f32[40,40,128]{2,1,0:T(8,128)} %divide_multiply_fusion.kern_ref, bf16[40,80]{1,0:T(8,128)(2,1)} %constant.54.clone.left_ref, ...), custom_call_target="tpu_custom_call" | custom-call | flops 200000000 | bytes 2000000 | tf_op jit(solution)/shard_map/exchange/pallas_call | solution.py:140
  21.8 0.5 broadcast.153
  22.3 1.6 %reduce.3 = bf16[32,2000]{1,0:T(8,128)(2,1)S(1)} reduce(bf16[32,1,2000]{2,0,1:T(8,128)(2,1)} %bitcast.2, bf16[]{:T(256)} %broadcast.153), dimensions={1}, to_apply=%copy.6.reduce_sub_computation | reduce | bytes 256002 | tf_op jit(solution)/shard_map/all_to_all | solution.py:164
  23.9 0.2 reshape.93
  24.1 34.9 %all_to_all.9 = bf16[32,2,1000]{2,1,0:T(2,128)(2,1)S(1)} all-to-all(bf16[32,2,1000]{2,1,0:T(2,128)(2,1)S(1)} %reshape.93), channel_id=1, replica_groups=mesh['wide'=32,'blk'=16] {'wide'}, dimensions={0} | all-to-all | bytes 256000 | tf_op jit(solution)/shard_map/all_to_all | solution.py:164
  59.0 0.2 reshape.94
  59.2 0.8 %convert_reduce_fusion = f32[2000]{0:T(1024)} fusion(bf16[32,1,2000]{2,1,0:T(2,128)(2,1)S(1)} %reshape.94), kind=kLoop, calls=%fused_computation.1 | loop fusion | flops 126000 | bytes 136000 | tf_op jit(solution)/shard_map/reduce_sum | solution.py:165
  (2 shorter events, 0.0 us)
Async XLA Ops:
  0.0 6.0 %copy-start.1 = (bf16[1,64000]{1,0:T(2,128)(2,1)S(1)}, bf16[1,64000]{1,0:T(2,128)(2,1)}, u32[]{:S(2)}) copy-start(bf16[1,64000]{1,0:T(2,128)(2,1)} %param.6) | copy-start | bytes 384004
  1.9 4.8 %copy-start = (bf16[32,2000]{1,0:T(8,128)(2,1)}, bf16[32,2000]{1,0:T(8,128)(2,1)S(1)}, u32[]{:S(2)}) copy-start(bf16[32,2000]{1,0:T(8,128)(2,1)S(1)} %reshape.89.s0_ref) | copy-start | bytes 384004
  1.9 11.9 %collective-permute-start = (bf16[32,2000]{1,0:T(8,128)(2,1)S(1)}, bf16[32,2000]{1,0:T(8,128)(2,1)S(1)}, u32[]{:S(2)}, u32[]{:S(2)}) collective-permute-start(bf16[32,2000]{1,0:T(8,128)(2,1)S(1)} %reshape.89.s0_ref), channel_id=1, source_target_pairs={{15,0},{0,1},{1,2},{2,3},{3,4},{4,5},{5,6},{6,7},{7,8},{8,9},{9,10... | collective-permute-start | bytes 384008 | tf_op jit(solution)/shard_map/ppermute | solution.py:156
  7.0 9.8 %collective-permute-start.1 = (bf16[32,2000]{1,0:T(8,128)(2,1)S(1)}, bf16[32,2000]{1,0:T(8,128)(2,1)S(1)}, u32[]{:S(2)}, u32[]{:S(2)}) collective-permute-start(bf16[32,2000]{1,0:T(8,128)(2,1)S(1)} %reshape.90), channel_id=1, source_target_pairs={{15,0},{0,1},{1,2},{2,3},{3,4},{4,5},{5,6},{6,7},{7,8},{8,9},{9,10... | collective-permute-start | bytes 384008 | tf_op jit(solution)/shard_map/ppermute | solution.py:156
  13.8 2.9 %copy-start.2 = (bf16[32,2000]{1,0:T(8,128)(2,1)}, bf16[32,2000]{1,0:T(8,128)(2,1)S(1)}, u32[]{:S(2)}) copy-start(bf16[32,2000]{1,0:T(8,128)(2,1)S(1)} %collective-permute-done.s1_ref) | copy-start | bytes 384004
  16.7 0.6 %copy-start.3 = (bf16[32,2000]{1,0:T(8,128)(2,1)}, bf16[32,2000]{1,0:T(8,128)(2,1)S(1)}, u32[]{:S(2)}) copy-start(bf16[32,2000]{1,0:T(8,128)(2,1)S(1)} %collective-permute-done.1.t_ref) | copy-start | bytes 384004

commit v2 on v1

v2 whole, which is shorter than its diff:
```python
import math

import jax
import jax.numpy as jnp
import numpy as np
from jax import lax
from jax.experimental import pallas as pl
from jax.experimental.pallas import tpu as pltpu
from jax.sharding import PartitionSpec as P

GRID = 40
ROWS = GRID * GRID
LANES = 128
HALF = 64
PIECES = 32
PIECE = GRID**3 // PIECES
GROUPS = PIECE // GRID
SCREEN = 0.3


def tables():
    index = np.arange(GRID)
    product = index[:, None] * index[None, :] % GRID
    folded = np.minimum(product, GRID - product)
    angle = 2.0 * math.pi / GRID * folded
    cos = np.cos(angle)
    sin = np.where(product <= GRID // 2, 1.0, -1.0) * np.sin(angle)
    sin = np.where((product == 0) | (product == GRID // 2), 0.0, sin)
    return cos.astype(np.float32), sin.astype(np.float32)


def weights():
    cos, sin = tables()

    def left(sign):
        return np.block([[cos, sign * sin], [-sign * sin, cos]])

    spread = np.zeros((2 * LANES, LANES), np.float32)
    first = np.zeros((LANES, 2 * LANES), np.float32)
    for row, col, table in ((0, 0, cos), (0, 1, -sin), (1, 0, sin), (1, 1, cos)):
        first[row * HALF : row * HALF + GRID, col * LANES : col * LANES + GRID] = table
    for row, col, table in ((0, 0, cos), (0, 1, sin), (1, 0, -sin), (1, 1, cos)):
        spread[row * LANES : row * LANES + GRID, col * HALF : col * HALF + GRID] = table
    return left(1.0), left(-1.0), first, spread


def kernel_table():
    index = jnp.arange(GRID, dtype=jnp.int32)
    wrapped = (index + GRID // 2) % GRID - GRID // 2
    wave = 2.0 * math.pi / GRID * wrapped.astype(jnp.float32)
    square = wave * wave
    lane = jnp.arange(LANES, dtype=jnp.int32) % GRID
    lane_wrapped = (lane + GRID // 2) % GRID - GRID // 2
    lane_wave = 2.0 * math.pi / GRID * lane_wrapped.astype(jnp.float32)
    lane_square = lane_wave * lane_wave
    total = square[None, :, None] + square[:, None, None] + lane_square[None, None, :]
    return 4.0 * math.pi / (total + SCREEN * SCREEN) / float(GRID**3)


def body(s0_ref, s1_ref, t_ref, kern_ref, fwd_ref, inv_ref, first_ref, last_ref, out_ref, xs, real, imag, flat, sums):
    lane = lax.broadcasted_iota(jnp.int32, (PIECES, LANES), 1)
    low = lane < HALF
    wide = flat.shape[2]

    target = t_ref[...]
    flat[0, :, :PIECE] = s0_ref[...] * target
    flat[1, :, :PIECE] = s1_ref[...] * target
    flat[:, :, PIECE:] = jnp.zeros((2, PIECES, wide - PIECE), jnp.bfloat16)

    def aligned(which, group, to):
        start = GRID * group
        tile, shift = start // LANES, start % LANES
        value = flat[which, :, tile * LANES : (tile + 1) * LANES]
        if shift + GRID > LANES:
            after = flat[which, :, (tile + 1) * LANES : (tile + 2) * LANES]
            value = jnp.where(lane >= shift, value, after)
        turn = (to - shift) % LANES
        return pltpu.roll(value, turn, 1) if turn else value

    for group in range(GROUPS):
        merged = jnp.where(low, aligned(0, group, 0), aligned(1, group, HALF))
        xs[pl.ds(group, PIECES, stride=GROUPS), :] = merged.astype(jnp.float32)

    forward, inverse = fwd_ref[...], inv_ref[...]
    re, im = slice(0, LANES), slice(LANES, 2 * LANES)

    def turned(table, first, second):
        both = jnp.concatenate([first, second], axis=1).astype(jnp.bfloat16)
        return jnp.dot(table, both, preferred_element_type=jnp.float32)

    def stacked(rows):
        return jnp.concatenate([real[rows, :], imag[rows, :]], axis=0)

    def put(rows, value):
        real[rows, :] = value[:GRID]
        imag[rows, :] = value[GRID:]

    def along_b(table):
        for pair in range(GRID // 2):
            one, two = pl.ds(2 * pair * GRID, GRID), pl.ds((2 * pair + 1) * GRID, GRID)
            value = turned(table, stacked(one), stacked(two))
            put(one, value[:, re])
            put(two, value[:, im])

    spread = jnp.dot(xs[...].astype(jnp.bfloat16), first_ref[...], preferred_element_type=jnp.float32)
    real[...] = spread[:, re]
    imag[...] = spread[:, im]
    along_b(forward)
    for pair in range(GRID // 2):
        one, two = pl.ds(2 * pair, GRID, stride=GRID), pl.ds(2 * pair + 1, GRID, stride=GRID)
        value = turned(forward, stacked(one), stacked(two))
        scale = [jnp.concatenate([kern_ref[2 * pair + which]] * 2, axis=0) for which in range(2)]
        value = turned(inverse, value[:, re] * scale[0], value[:, im] * scale[1])
        put(one, value[:, re])
        put(two, value[:, im])
    along_b(inverse)
    both = jnp.concatenate([real[...], imag[...]], axis=1).astype(jnp.bfloat16)
    xs[...] = jnp.dot(both, last_ref[...], preferred_element_type=jnp.float32)

    tiles = [[None] * (wide // LANES) for _ in range(2)]
    for group in range(GROUPS):
        start = GRID * group
        tile, shift = start // LANES, start % LANES
        value = xs[pl.ds(group, PIECES, stride=GROUPS), :].astype(jnp.bfloat16)
        for which in range(2):
            turn = (shift - HALF * which) % LANES
            moved = pltpu.roll(value, turn, 1) if turn else value
            held = tiles[which][tile]
            tiles[which][tile] = moved if held is None else jnp.where(lane >= shift, moved, held)
            if shift + GRID > LANES:
                tiles[which][tile + 1] = moved
    for tile in range(wide // LANES):
        size = min(LANES, PIECE - tile * LANES)
        here = slice(tile * LANES, tile * LANES + size)
        total = s0_ref[:, here].astype(jnp.float32) * tiles[0][tile][:, :size].astype(jnp.float32)
        total += s1_ref[:, here].astype(jnp.float32) * tiles[1][tile][:, :size].astype(jnp.float32)
        sums[pl.ds(tile, PIECES, stride=wide // LANES), :size] = -total
    out_ref[...] = sums[...].astype(jnp.bfloat16)


def exchange_term(s0, s1, target):
    tables_in = [jnp.asarray(w, jnp.bfloat16) for w in weights()]
    tiles = -(-PIECE // LANES)
    vmem = pl.BlockSpec(memory_space=pltpu.VMEM)
    return pl.pallas_call(
        body,
        out_shape=jax.ShapeDtypeStruct((PIECES * tiles, LANES), jnp.bfloat16),
        in_specs=[vmem] * 8,
        out_specs=vmem,
        scratch_shapes=[
            pltpu.VMEM((ROWS, LANES), jnp.float32),
            pltpu.VMEM((ROWS, LANES), jnp.float32),
            pltpu.VMEM((ROWS, LANES), jnp.float32),
            pltpu.VMEM((2, PIECES, tiles * LANES), jnp.bfloat16),
            pltpu.VMEM((PIECES * tiles, LANES), jnp.float32),
        ],
        compiler_params=pltpu.CompilerParams(vmem_limit_bytes=16 * 2**20),
        cost_estimate=pl.CostEstimate(flops=200_000_000, bytes_accessed=2_000_000, transcendentals=0),
        name="exchange",
    )(s0, s1, target, kernel_table(), *tables_in)


def from_behind(block):
    count = lax.axis_size("blk")
    return lax.ppermute(block, "blk", [((i - 1) % count, i) for i in range(count)])


def shards(sources, targets):
    own = sources.reshape(PIECES, PIECE)
    target = from_behind(targets.reshape(PIECES, PIECE))
    behind = from_behind(own)
    partial = exchange_term(own, behind, target)
    arrived = lax.all_to_all(partial, "wide", split_axis=0, concat_axis=0, tiled=True)
    summed = arrived.reshape(PIECES, -1, LANES).astype(jnp.float32).sum(axis=0)
    return summed.reshape(1, -1)[:, :PIECE]


def solution(mesh):
    in_specs = (P(("wide", "blk"), None), P("blk", None))
    return jax.shard_map(shards, mesh=mesh, in_specs=in_specs, out_specs=P("blk", "wide"), check_vma=False)
```

time: 60.2 us -> 54.9 us (0.912)
  other arithmetic: 6.15 us -> 3.48 us
  Pallas kernels: 4.43 us -> 2.45 us
  local copies, waits for them, and re-layouts: 1.94 us -> 0.45 us
  waiting for transfers between devices: 5.27 us -> 6.12 us
    pallas_call x1, Pallas kernels: 4.43 us -> 2.45 us  [exchange_term(): pl.pallas_call(body, out_shape=jax.ShapeDtypeStruct((PIECES * tiles, LANE...]
    all_to_all x1 -> x0, other arithmetic: 1.58 us -> none  [shards(): lax.all_to_all(partial, 'wide', split_axis=0, concat_axis=0, tiled=True)]
    unnamed x10, local copies, waits for them, and re-layouts: 1 us -> 0.02 us
    div x1, other arithmetic: 1.18 us -> 0.29 us  [kernel_table(): return 4.0 * math.pi / (total + SCREEN * SCREEN) / float(GRID ** 3)]
    ppermute x2, waiting for transfers between devices: 5.27 us -> 6.12 us  [from_behind(): lax.ppermute(block, 'blk', [((i - 1) % count, i) for i in range(count)])]
  transfers between devices with their start and end apart: 2 -> 2, of which waited for: 2 -> 2; matrix products, arithmetic and copies ran while one was open for 4% -> 2% of each run, Pallas kernels for 0% -> 0%
where the time goes in v2:
time: 54.9 us; the launch traced here: 54.7 us
  blocking collectives  34.9 us (64%)
  starting transfers between devices  7.23 us (13%)
  waiting for transfers between devices  6.12 us (11%)
  other arithmetic  3.48 us (6%)
  Pallas kernels  2.45 us (4%)
    all_to_all x1, blocking collectives, shards(): lax.all_to_all(partial, 'wide', split_axis=0, concat_axis=0, tiled=True)  34.9 us
    ppermute x2, starting transfers between devices, from_behind(): lax.ppermute(block, 'blk', [((i - 1) % count, i) for i in range(count)])  7.23 us
    ppermute x2, waiting for transfers between devices, from_behind(): lax.ppermute(block, 'blk', [((i - 1) % count, i) for i in range(count)])  6.12 us
    pallas_call x1, Pallas kernels, exchange_term(): pl.pallas_call(body, out_shape=jax.ShapeDtypeStruct((PIECES * tiles, LANE...  2.45 us
    unnamed x2, other arithmetic  2.45 us
  transfers between devices with their start and end apart: 2, of which 2 were waited for; matrix products, arithmetic and copies ran while one was open for 2% of the time, Pallas kernels for 0%

profile of v2, /device:TPU:1, one launch (start us, length us, event | category | flops | bytes accessed | tf_op | source)
XLA Modules:
  0.0 54.7 jit_solution(6338716163921092045)
XLA Ops:
  0.0 0.0 copy-start.4
  0.0 1.7 %reduce.1 = bf16[64000]{0:T(1024)(128)(2,1)S(1)} reduce(bf16[1,64000]{1,0:T(2,128)(2,1)} %param.7, bf16[]{:T(256)} %constant.53), dimensions={0}, to_apply=%param.7.reduce_sub_computation | reduce | bytes 256002 | tf_op args[1]
  1.7 0.2 reshape.94
  1.9 4.0 %collective-permute-start.1 = (bf16[32,2000]{1,0:T(8,128)(2,1)S(1)}, bf16[32,2000]{1,0:T(8,128)(2,1)S(1)}, u32[]{:S(2)}, u32[]{:S(2)}) collective-permute-start(bf16[32,2000]{1,0:T(8,128)(2,1)S(1)} %reshape.94), channel_id=1, source_target_pairs={{15,0},{0,1},{1,2},{2,3},{3,4},{4,5},{5,6},{6,7},{7,8},{8,9},{9,10... | collective-permute-start | bytes 384008 | tf_op jit(solution)/shard_map/ppermute | solution.py:165
  6.0 0.0 copy-done.4
  6.0 0.7 %reduce = bf16[64000]{0:T(1024)(128)(2,1)S(1)} reduce(bf16[1,64000]{1,0:T(2,128)(2,1)S(1)} %copy-done.4, bf16[]{:T(256)} %constant.53), dimensions={0}, to_apply=%param.6.reduce_sub_computation | reduce | bytes 256002 | tf_op args[0]
  6.7 0.2 reshape.93.s0_ref
  6.9 3.2 %collective-permute-start = (bf16[32,2000]{1,0:T(8,128)(2,1)S(1)}, bf16[32,2000]{1,0:T(8,128)(2,1)S(1)}, u32[]{:S(2)}, u32[]{:S(2)}) collective-permute-start(bf16[32,2000]{1,0:T(8,128)(2,1)S(1)} %reshape.93.s0_ref), channel_id=1, source_target_pairs={{15,0},{0,1},{1,2},{2,3},{3,4},{4,5},{5,6},{6,7},{7,8},{8,9},{9,10... | collective-permute-start | bytes 384008 | tf_op jit(solution)/shard_map/ppermute | solution.py:165
  10.2 0.1 broadcast_add_fusion
  10.3 0.0 copy-start
  10.3 0.0 copy-start.1
  10.3 0.0 copy-start.2
  10.3 0.0 copy-start.3
  10.3 0.3 divide_multiply_fusion.kern_ref
  10.6 3.2 %collective-permute-done.1.t_ref = bf16[32,2000]{1,0:T(8,128)(2,1)S(1)} collective-permute-done((bf16[32,2000]{1,0:T(8,128)(2,1)S(1)}, bf16[32,2000]{1,0:T(8,128)(2,1)S(1)}, u32[]{:S(2)}, u32[]{:S(2)}) %collective-permute-start.1) | collective-permute-done | bytes 128032 | tf_op jit(solution)/shard_map/ppermute | solution.py:165
  13.8 2.9 %collective-permute-done.s1_ref = bf16[32,2000]{1,0:T(8,128)(2,1)S(1)} collective-permute-done((bf16[32,2000]{1,0:T(8,128)(2,1)S(1)}, bf16[32,2000]{1,0:T(8,128)(2,1)S(1)}, u32[]{:S(2)}, u32[]{:S(2)}) %collective-permute-start) | collective-permute-done | bytes 128032 | tf_op jit(solution)/shard_map/ppermute | solution.py:165
  16.7 0.0 copy-done
  16.7 0.0 copy-done.1
  16.7 0.0 copy-done.2
  16.7 0.0 copy-done.3
  16.7 2.4 %exchange.1 = bf16[512,128]{1,0:T(8,128)(2,1)S(1)} custom-call(bf16[32,2000]{1,0:T(8,128)(2,1)S(1)} %reshape.93.s0_ref, bf16[32,2000]{1,0:T(8,128)(2,1)S(1)} %collective-permute-done.s1_ref, bf16[32,2000]{1,0:T(8,128)(2,1)S(1)} %collective-permute-done.1.t_ref, f32[40,40,128]{2,1,0:T(8,128)S(1)} %divide_multiply_fusion.kern_ref, ...), custom_call_target="tpu_custom_call" | custom-call | flops 200000000 | bytes 2000000 | tf_op jit(solution)/shard_map/exchange/pallas_call | solution.py:145
  19.2 34.9 %all_to_all.9 = bf16[32,16,128]{2,1,0:T(8,128)(2,1)S(1)} all-to-all(bf16[32,16,128]{2,1,0:T(8,128)(2,1)S(1)} %bitcast.3), channel_id=1, replica_groups=mesh['wide'=32,'blk'=16] {'wide'}, dimensions={0} | all-to-all | bytes 262144 | tf_op jit(solution)/shard_map/all_to_all | solution.py:173
  54.1 0.6 %convert_reduce_fusion = f32[16,128]{1,0:T(8,128)} fusion(bf16[32,16,128]{2,1,0:T(8,128)(2,1)S(1)} %all_to_all.9), kind=kLoop, calls=%fused_computation.1 | loop fusion | flops 129024 | bytes 139264 | tf_op jit(solution)/shard_map/reduce_sum | solution.py:174
  (2 shorter events, 0.0 us)
Async XLA Ops:
  0.0 6.0 %copy-start.4 = (bf16[1,64000]{1,0:T(2,128)(2,1)S(1)}, bf16[1,64000]{1,0:T(2,128)(2,1)}, u32[]{:S(2)}) copy-start(bf16[1,64000]{1,0:T(2,128)(2,1)} %param.6) | copy-start | bytes 384004
  1.9 11.9 %collective-permute-start.1 = (bf16[32,2000]{1,0:T(8,128)(2,1)S(1)}, bf16[32,2000]{1,0:T(8,128)(2,1)S(1)}, u32[]{:S(2)}, u32[]{:S(2)}) collective-permute-start(bf16[32,2000]{1,0:T(8,128)(2,1)S(1)} %reshape.94), channel_id=1, source_target_pairs={{15,0},{0,1},{1,2},{2,3},{3,4},{4,5},{5,6},{6,7},{7,8},{8,9},{9,10... | collective-permute-start | bytes 384008 | tf_op jit(solution)/shard_map/ppermute | solution.py:165
  6.9 9.8 %collective-permute-start = (bf16[32,2000]{1,0:T(8,128)(2,1)S(1)}, bf16[32,2000]{1,0:T(8,128)(2,1)S(1)}, u32[]{:S(2)}, u32[]{:S(2)}) collective-permute-start(bf16[32,2000]{1,0:T(8,128)(2,1)S(1)} %reshape.93.s0_ref), channel_id=1, source_target_pairs={{15,0},{0,1},{1,2},{2,3},{3,4},{4,5},{5,6},{6,7},{7,8},{8,9},{9,10... | collective-permute-start | bytes 384008 | tf_op jit(solution)/shard_map/ppermute | solution.py:165
  10.3 6.4 %copy-start = (bf16[256,128]{1,0:T(8,128)(2,1)S(1)}, bf16[256,128]{1,0:T(8,128)(2,1)}, u32[]{:S(2)}) copy-start(bf16[256,128]{1,0:T(8,128)(2,1)} %constant.50.clone.last_ref) | copy-start | bytes 196612
  10.3 6.4 %copy-start.1 = (bf16[128,256]{1,0:T(8,128)(2,1)S(1)}, bf16[128,256]{1,0:T(8,128)(2,1)}, u32[]{:S(2)}) copy-start(bf16[128,256]{1,0:T(8,128)(2,1)} %constant.49.clone.first_ref) | copy-start | bytes 196612
  10.3 6.4 %copy-start.2 = (bf16[80,80]{1,0:T(8,128)(2,1)S(1)}, bf16[80,80]{1,0:T(8,128)(2,1)}, u32[]{:S(2)}) copy-start(bf16[80,80]{1,0:T(8,128)(2,1)} %constant.48.clone.inv_ref) | copy-start | bytes 38404
  10.3 6.4 %copy-start.3 = (bf16[80,80]{1,0:T(8,128)(2,1)S(1)}, bf16[80,80]{1,0:T(8,128)(2,1)}, u32[]{:S(2)}) copy-start(bf16[80,80]{1,0:T(8,128)(2,1)} %constant.47.clone.fwd_ref) | copy-start | bytes 38404

commit v3 on v2

--- a/solution.py
+++ b/solution.py
@@ -15,6 +15,11 @@
 PIECES = 32
 PIECE = GRID**3 // PIECES
 GROUPS = PIECE // GRID
+TILES = -(-PIECE // LANES)
+WIDE = TILES * LANES
+FLAT = GRID**3 // LANES
+CYCLE = 8
+BLOCK = 8
 SCREEN = 0.3
 
 
@@ -57,15 +62,32 @@
     return 4.0 * math.pi / (total + SCREEN * SCREEN) / float(GRID**3)
 
 
-def body(s0_ref, s1_ref, t_ref, kern_ref, fwd_ref, inv_ref, first_ref, last_ref, out_ref, xs, real, imag, flat, sums):
+def gather_body(s_ref, t_ref, out_ref, rows, pieces):
+    lane = lax.broadcasted_iota(jnp.int32, (PIECES // CYCLE, LANES), 1)
+    period = CYCLE * PIECE // LANES
+    for which, ref in enumerate((s_ref, t_ref)):
+        rows[:FLAT, :] = ref[...].astype(jnp.float32).reshape(FLAT, LANES)
+        rows[FLAT:, :] = jnp.zeros((rows.shape[0] - FLAT, LANES), jnp.float32)
+        for piece in range(CYCLE):
+            for tile in range(TILES):
+                row, shift = divmod(PIECE * piece + LANES * tile, LANES)
+                value = rows[pl.ds(row, PIECES // CYCLE, stride=period), :]
+                if shift:
+                    after = rows[pl.ds(row + 1, PIECES // CYCLE, stride=period), :]
+                    value = pltpu.roll(jnp.where(lane >= shift, value, after), LANES - shift, 1)
+                start = which * PIECES + piece
+                pieces[tile, pl.ds(start, PIECES // CYCLE, stride=CYCLE), :] = value
+    for tile in range(TILES):
+        out_ref[:, tile * LANES : (tile + 1) * LANES] = pieces[tile].astype(jnp.bfloat16)
+
+
+def body(own_ref, came_ref, kern_ref, fwd_ref, inv_ref, first_ref, last_ref, out_ref, xs, real, imag, flat, sums):
     lane = lax.broadcasted_iota(jnp.int32, (PIECES, LANES), 1)
     low = lane < HALF
-    wide = flat.shape[2]
-
-    target = t_ref[...]
-    flat[0, :, :PIECE] = s0_ref[...] * target
-    flat[1, :, :PIECE] = s1_ref[...] * target
-    flat[:, :, PIECE:] = jnp.zeros((2, PIECES, wide - PIECE), jnp.bfloat16)
+
+    target = came_ref[PIECES:, :]
+    flat[0] = own_ref[:PIECES, :] * target
+    flat[1] = came_ref[:PIECES, :] * target
 
     def aligned(which, group, to):
         start = GRID * group
@@ -117,7 +139,7 @@
     both = jnp.concatenate([real[...], imag[...]], axis=1).astype(jnp.bfloat16)
     xs[...] = jnp.dot(both, last_ref[...], preferred_element_type=jnp.float32)
 
-    tiles = [[None] * (wide // LANES) for _ in range(2)]
+    tiles = [[None] * TILES for _ in range(2)]
     for group in range(GROUPS):
         start = GRID * group
         tile, shift = start // LANES, start % LANES
@@ -129,47 +151,67 @@
             tiles[which][tile] = moved if held is None else jnp.where(lane >= shift, moved, held)
             if shift + GRID > LANES:
                 tiles[which][tile + 1] = moved
-    for tile in range(wide // LANES):
-        size = min(LANES, PIECE - tile * LANES)
-        here = slice(tile * LANES, tile * LANES + size)
-        total = s0_ref[:, here].astype(jnp.float32) * tiles[0][tile][:, :size].astype(jnp.float32)
-        total += s1_ref[:, here].astype(jnp.float32) * tiles[1][tile][:, :size].astype(jnp.float32)
-        sums[pl.ds(tile, PIECES, stride=wide // LANES), :size] = -total
+    for tile in range(TILES):
+        here = slice(tile * LANES, (tile + 1) * LANES)
+        total = own_ref[:PIECES, here].astype(jnp.float32) * tiles[0][tile].astype(jnp.float32)
+        total += came_ref[:PIECES, here].astype(jnp.float32) * tiles[1][tile].astype(jnp.float32)
+        sums[pl.ds(tile, PIECES, stride=TILES), :] = -total
     out_ref[...] = sums[...].astype(jnp.bfloat16)
 
 
-def exchange_term(s0, s1, target):
-    tables_in = [jnp.asarray(w, jnp.bfloat16) for w in weights()]
-    tiles = -(-PIECE // LANES)
-    vmem = pl.BlockSpec(memory_space=pltpu.VMEM)
+VMEM = pl.BlockSpec(memory_space=pltpu.VMEM)
+PARAMS = pltpu.CompilerParams(vmem_limit_bytes=16 * 2**20)
+
+
+def gathered(sources, targets):
+    return pl.pallas_call(
+        gather_body,
+        out_shape=jax.ShapeDtypeStruct((2 * PIECES, WIDE), jnp.bfloat16),
+        in_specs=[VMEM] * 2,
+        out_specs=VMEM,
+        scratch_shapes=[
+            pltpu.VMEM((FLAT + 4, LANES), jnp.float32),
+            pltpu.VMEM((TILES, 2 * PIECES, LANES), jnp.float32),
+        ],
+        compiler_params=PARAMS,
+        cost_estimate=pl.CostEstimate(flops=1_000_000, bytes_accessed=800_000, transcendentals=0),
+        name="gather",
+    )(sources, targets)
+
+
+def exchange_term(own, came):
+    constants = [jnp.asarray(w, jnp.bfloat16) for w in weights()]
     return pl.pallas_call(
         body,
-        out_shape=jax.ShapeDtypeStruct((PIECES * tiles, LANES), jnp.bfloat16),
-        in_specs=[vmem] * 8,
-        out_specs=vmem,
+        out_shape=jax.ShapeDtypeStruct((PIECES * TILES, LANES), jnp.bfloat16),
+        in_specs=[VMEM] * 7,
+        out_specs=VMEM,
         scratch_shapes=[
             pltpu.VMEM((ROWS, LANES), jnp.float32),
             pltpu.VMEM((ROWS, LANES), jnp.float32),
             pltpu.VMEM((ROWS, LANES), jnp.float32),
-            pltpu.VMEM((2, PIECES, tiles * LANES), jnp.bfloat16),
-            pltpu.VMEM((PIECES * tiles, LANES), jnp.float32),
+            pltpu.VMEM((2, PIECES, WIDE), jnp.bfloat16),
+            pltpu.VMEM((PIECES * TILES, LANES), jnp.float32),
         ],
-        compiler_params=pltpu.CompilerParams(vmem_limit_bytes=16 * 2**20),
+        compiler_params=PARAMS,
         cost_estimate=pl.CostEstimate(flops=200_000_000, bytes_accessed=2_000_000, transcendentals=0),
         name="exchange",
-    )(s0, s1, target, kernel_table(), *tables_in)
+    )(own, came, kernel_table(), *constants)
 
 
 def from_behind(block):
-    count = lax.axis_size("blk")
-    return lax.ppermute(block, "blk", [((i - 1) % count, i) for i in range(count)])
+    wide, blk = lax.axis_size("wide"), lax.axis_size("blk")
+
+    def source(w, b):
+        return w * blk + b - 1 if b else (w - BLOCK) % wide * blk + blk - 1
+
+    route = [(source(w, b), w * blk + b) for w in range(wide) for b in range(blk)]
+    return lax.ppermute(block, ("wide", "blk"), route)
 
 
 def shards(sources, targets):
-    own = sources.reshape(PIECES, PIECE)
-    target = from_behind(targets.reshape(PIECES, PIECE))
-    behind = from_behind(own)
-    partial = exchange_term(own, behind, target)
+    own = gathered(sources, targets)
+    partial = exchange_term(own, from_behind(own))
     arrived = lax.all_to_all(partial, "wide", split_axis=0, concat_axis=0, tiled=True)
     summed = arrived.reshape(PIECES, -1, LANES).astype(jnp.float32).sum(axis=0)
     return summed.reshape(1, -1)[:, :PIECE]

time: 54.9 us -> 53.7 us (0.978)
  waiting for transfers between devices: 6.12 us -> 15.9 us
  blocking collectives: 34.9 us -> 27.6 us
  starting transfers between devices: 7.23 us -> 4.02 us
  other arithmetic: 3.48 us -> 1.03 us
  local copies, waits for them, and re-layouts: 0.45 us -> 1.92 us
    ppermute x2 -> x1, waiting for transfers between devices: 6.12 us -> 15.9 us  [from_behind(): return lax.ppermute(block, ('wide', 'blk'), route)]
    all_to_all x1, blocking collectives: 34.9 us -> 27.6 us  [shards(): lax.all_to_all(partial, 'wide', split_axis=0, concat_axis=0, tiled=True)]
    ppermute x2 -> x1, starting transfers between devices: 7.23 us -> 4.02 us  [from_behind(): return lax.ppermute(block, ('wide', 'blk'), route)]
    unnamed x2 -> x0, other arithmetic: 2.45 us -> none
    unnamed x10 -> x12, local copies, waits for them, and re-layouts: 0.02 us -> 1.92 us
    pallas_call x1 -> x2, Pallas kernels: 2.45 us -> 2.81 us  [the longest x1 2.46 us: exchange_term(): pl.pallas_call(body, out_shape=jax.ShapeDtypeStruct((PIECES * TILES, LANE...]
  transfers between devices with their start and end apart: 2 -> 1, of which waited for: 2 -> 1; matrix products, arithmetic and copies ran while one was open for 2% -> 1% of each run, Pallas kernels for 0% -> 0%
where the time goes in v3:
time: 53.7 us; the launch traced here: 53.4 us
  blocking collectives  27.6 us (51%)
  waiting for transfers between devices  15.9 us (30%)
  starting transfers between devices  4.02 us (7%)
  Pallas kernels  2.81 us (5%)
  local copies, waits for them, and re-layouts  1.92 us (4%)
  other arithmetic  1.03 us (2%)
    all_to_all x1, blocking collectives, shards(): lax.all_to_all(partial, 'wide', split_axis=0, concat_axis=0, tiled=True)  27.6 us
    ppermute x1, waiting for transfers between devices, from_behind(): return lax.ppermute(block, ('wide', 'blk'), route)  15.9 us
    ppermute x1, starting transfers between devices, from_behind(): return lax.ppermute(block, ('wide', 'blk'), route)  4.02 us
    pallas_call x1, Pallas kernels, exchange_term(): pl.pallas_call(body, out_shape=jax.ShapeDtypeStruct((PIECES * TILES, LANE...  2.46 us
    unnamed x12, local copies, waits for them, and re-layouts  1.92 us
  transfers between devices with their start and end apart: 1, of which 1 were waited for; matrix products, arithmetic and copies ran while one was open for 1% of the time, Pallas kernels for 0%

profile of v3, /device:TPU:1, one launch (start us, length us, event | category | flops | bytes accessed | tf_op | source)
XLA Modules:
  0.0 53.4 jit_solution(17355011208486942810)
XLA Ops:
  0.0 0.0 copy-start
  0.0 0.9 %copy-done = bf16[1,64000]{1,0:T(2,128)(2,1)S(1)} copy-done((bf16[1,64000]{1,0:T(2,128)(2,1)S(1)}, bf16[1,64000]{1,0:T(2,128)(2,1)}, u32[]{:S(2)}) %copy-start) | copy-done | bytes 128024
  0.9 0.0 copy-start.1
  1.0 0.9 %copy-done.1 = bf16[1,64000]{1,0:T(2,128)(2,1)S(1)} copy-done((bf16[1,64000]{1,0:T(2,128)(2,1)S(1)}, bf16[1,64000]{1,0:T(2,128)(2,1)}, u32[]{:S(2)}) %copy-start.1) | copy-done | bytes 128024
  1.9 0.4 gather.1.own_ref
  2.3 4.0 %collective-permute-start = (bf16[64,2048]{1,0:T(8,128)(2,1)S(1)}, bf16[64,2048]{1,0:T(8,128)(2,1)S(1)}, u32[]{:S(2)}, u32[]{:S(2)}) collective-permute-start(bf16[64,2048]{1,0:T(8,128)(2,1)S(1)} %gather.1.own_ref), channel_id=1, source_target_pairs={{399,0},{0,1},{1,2},{2,3},{3,4},{4,5},{5,6},{6,7},{7,8},{8,9},{9,1... | collective-permute-start | bytes 786440 | tf_op jit(solution)/shard_map/ppermute | solution.py:209
  6.3 0.1 broadcast_add_fusion
  6.4 0.0 copy-start.2
  6.4 0.0 copy-start.3
  6.4 0.0 copy-start.4
  6.4 0.0 copy-start.5
  6.5 0.3 divide_multiply_fusion.kern_ref
  6.7 15.9 %collective-permute-done.came_ref = bf16[64,2048]{1,0:T(8,128)(2,1)S(1)} collective-permute-done((bf16[64,2048]{1,0:T(8,128)(2,1)S(1)}, bf16[64,2048]{1,0:T(8,128)(2,1)S(1)}, u32[]{:S(2)}, u32[]{:S(2)}) %collective-permute-start) | collective-permute-done | bytes 262176 | tf_op jit(solution)/shard_map/ppermute | solution.py:209
  22.7 0.0 copy-done.2
  22.7 0.0 copy-done.3
  22.7 0.0 copy-done.4
  22.7 0.0 copy-done.5
  22.7 2.5 %exchange.1 = bf16[512,128]{1,0:T(8,128)(2,1)S(1)} custom-call(bf16[64,2048]{1,0:T(8,128)(2,1)S(1)} %gather.1.own_ref, bf16[64,2048]{1,0:T(8,128)(2,1)S(1)} %collective-permute-done.came_ref, f32[40,40,128]{2,1,0:T(8,128)S(1)} %divide_multiply_fusion.kern_ref, bf16[80,80]{1,0:T(8,128)(2,1)S(1)} %copy-done.5, bf16[80,80]{1,0:T(8,128)(2,1)S(1)} %copy-done.4, ...), custom_call_target="tpu_custom_call" | custom-call | flops 200000000 | bytes 2000000 | tf_op jit(solution)/shard_map/exchange/pallas_call | solution.py:184
  25.1 27.6 %all_to_all.9 = bf16[32,16,128]{2,1,0:T(8,128)(2,1)S(1)} all-to-all(bf16[32,16,128]{2,1,0:T(8,128)(2,1)S(1)} %bitcast.3), channel_id=1, replica_groups=mesh['wide'=32,'blk'=16] {'wide'}, dimensions={0} | all-to-all | bytes 262144 | tf_op jit(solution)/shard_map/all_to_all | solution.py:215
  52.8 0.6 %convert_reduce_fusion = f32[16,128]{1,0:T(8,128)} fusion(bf16[32,16,128]{2,1,0:T(8,128)(2,1)S(1)} %all_to_all.9), kind=kLoop, calls=%fused_computation.1 | loop fusion | flops 129024 | bytes 139264 | tf_op jit(solution)/shard_map/reduce_sum | solution.py:216
  (2 shorter events, 0.0 us)
Async XLA Ops:
  0.0 0.9 %copy-start = (bf16[1,64000]{1,0:T(2,128)(2,1)S(1)}, bf16[1,64000]{1,0:T(2,128)(2,1)}, u32[]{:S(2)}) copy-start(bf16[1,64000]{1,0:T(2,128)(2,1)} %s_ref.1) | copy-start | bytes 384004
  0.9 0.9 %copy-start.1 = (bf16[1,64000]{1,0:T(2,128)(2,1)S(1)}, bf16[1,64000]{1,0:T(2,128)(2,1)}, u32[]{:S(2)}) copy-start(bf16[1,64000]{1,0:T(2,128)(2,1)} %t_ref.1) | copy-start | bytes 384004
  2.3 20.4 %collective-permute-start = (bf16[64,2048]{1,0:T(8,128)(2,1)S(1)}, bf16[64,2048]{1,0:T(8,128)(2,1)S(1)}, u32[]{:S(2)}, u32[]{:S(2)}) collective-permute-start(bf16[64,2048]{1,0:T(8,128)(2,1)S(1)} %gather.1.own_ref), channel_id=1, source_target_pairs={{399,0},{0,1},{1,2},{2,3},{3,4},{4,5},{5,6},{6,7},{7,8},{8,9},{9,1... | collective-permute-start | bytes 786440 | tf_op jit(solution)/shard_map/ppermute | solution.py:209
  6.4 16.3 %copy-start.2 = (bf16[256,128]{1,0:T(8,128)(2,1)S(1)}, bf16[256,128]{1,0:T(8,128)(2,1)}, u32[]{:S(2)}) copy-start(bf16[256,128]{1,0:T(8,128)(2,1)} %constant.50.clone.last_ref) | copy-start | bytes 196612
  6.4 16.2 %copy-start.3 = (bf16[128,256]{1,0:T(8,128)(2,1)S(1)}, bf16[128,256]{1,0:T(8,128)(2,1)}, u32[]{:S(2)}) copy-start(bf16[128,256]{1,0:T(8,128)(2,1)} %constant.49.clone.first_ref) | copy-start | bytes 196612
  6.4 16.2 %copy-start.4 = (bf16[80,80]{1,0:T(8,128)(2,1)S(1)}, bf16[80,80]{1,0:T(8,128)(2,1)}, u32[]{:S(2)}) copy-start(bf16[80,80]{1,0:T(8,128)(2,1)} %constant.48.clone.inv_ref) | copy-start | bytes 38404
  6.4 16.2 %copy-start.5 = (bf16[80,80]{1,0:T(8,128)(2,1)S(1)}, bf16[80,80]{1,0:T(8,128)(2,1)}, u32[]{:S(2)}) copy-start(bf16[80,80]{1,0:T(8,128)(2,1)} %constant.47.clone.fwd_ref) | copy-start | bytes 38404

commit v4 on v3

--- a/solution.py
+++ b/solution.py
@@ -7,6 +7,7 @@
 from jax.experimental import pallas as pl
 from jax.experimental.pallas import tpu as pltpu
 from jax.sharding import PartitionSpec as P
+
 
 GRID = 40
 ROWS = GRID * GRID
@@ -19,6 +20,8 @@
 WIDE = TILES * LANES
 FLAT = GRID**3 // LANES
 CYCLE = 8
+PARTS = 4
+ROUNDS = ({2: 0}, {3: 0}, {0: 3, 1: 0, 3: 1}, {0: 1}, {0: 2, 1: 3, 2: 1}, {3: 2}, {1: 2, 2: 3})
 BLOCK = 8
 SCREEN = 0.3
 
@@ -62,11 +65,20 @@
     return 4.0 * math.pi / (total + SCREEN * SCREEN) / float(GRID**3)
 
 
-def gather_body(s_ref, t_ref, out_ref, rows, pieces):
+def gather_body(s_ref, t_ref, out_ref, raw, rows, pieces, ready, arrived, left):
+    copies = []
+    for which, ref in enumerate((s_ref, t_ref)):
+        for part in range(PARTS):
+            here = pl.ds(part * GRID**3 // PARTS, GRID**3 // PARTS)
+            copies.append(pltpu.make_async_copy(ref.at[:, here], raw.at[which, :, here], arrived.at[which, part]))
+    for copy in copies:
+        copy.start()
     lane = lax.broadcasted_iota(jnp.int32, (PIECES // CYCLE, LANES), 1)
     period = CYCLE * PIECE // LANES
-    for which, ref in enumerate((s_ref, t_ref)):
-        rows[:FLAT, :] = ref[...].astype(jnp.float32).reshape(FLAT, LANES)
+    for which in range(2):
+        for copy in copies[which * PARTS : (which + 1) * PARTS]:
+            copy.wait()
+        rows[:FLAT, :] = raw[which].astype(jnp.float32).reshape(FLAT, LANES)
         rows[FLAT:, :] = jnp.zeros((rows.shape[0] - FLAT, LANES), jnp.float32)
         for piece in range(CYCLE):
             for tile in range(TILES):
@@ -75,10 +87,13 @@
                 if shift:
                     after = rows[pl.ds(row + 1, PIECES // CYCLE, stride=period), :]
                     value = pltpu.roll(jnp.where(lane >= shift, value, after), LANES - shift, 1)
-                start = which * PIECES + piece
-                pieces[tile, pl.ds(start, PIECES // CYCLE, stride=CYCLE), :] = value
-    for tile in range(TILES):
-        out_ref[:, tile * LANES : (tile + 1) * LANES] = pieces[tile].astype(jnp.bfloat16)
+                pieces[which, tile, pl.ds(piece, PIECES // CYCLE, stride=CYCLE), :] = value
+        for tile in range(TILES):
+            ready[which, :, tile * LANES : (tile + 1) * LANES] = pieces[which, tile].astype(jnp.bfloat16)
+        copies.append(pltpu.make_async_copy(ready.at[which], out_ref.at[pl.ds(which * PIECES, PIECES)], left.at[which]))
+        copies[-1].start()
+    for copy in copies[-2:]:
+        copy.wait()
 
 
 def body(own_ref, came_ref, kern_ref, fwd_ref, inv_ref, first_ref, last_ref, out_ref, xs, real, imag, flat, sums):
@@ -155,7 +170,8 @@
         here = slice(tile * LANES, (tile + 1) * LANES)
         total = own_ref[:PIECES, here].astype(jnp.float32) * tiles[0][tile].astype(jnp.float32)
         total += came_ref[:PIECES, here].astype(jnp.float32) * tiles[1][tile].astype(jnp.float32)
-        sums[pl.ds(tile, PIECES, stride=TILES), :] = -total
+        for part in range(PARTS):
+            sums[pl.ds(part * TILES + tile, BLOCK, stride=PARTS * TILES), :] = -total[part * BLOCK : (part + 1) * BLOCK]
     out_ref[...] = sums[...].astype(jnp.bfloat16)
 
 
@@ -167,13 +183,17 @@
     return pl.pallas_call(
         gather_body,
         out_shape=jax.ShapeDtypeStruct((2 * PIECES, WIDE), jnp.bfloat16),
-        in_specs=[VMEM] * 2,
-        out_specs=VMEM,
+        in_specs=[pl.BlockSpec(memory_space=pltpu.HBM)] * 2,
+        out_specs=pl.BlockSpec(memory_space=pltpu.HBM),
         scratch_shapes=[
+            pltpu.VMEM((2, 1, GRID**3), jnp.bfloat16),
             pltpu.VMEM((FLAT + 4, LANES), jnp.float32),
-            pltpu.VMEM((TILES, 2 * PIECES, LANES), jnp.float32),
+            pltpu.VMEM((2, TILES, PIECES, LANES), jnp.float32),
+            pltpu.VMEM((2, PIECES, WIDE), jnp.bfloat16),
+            pltpu.SemaphoreType.DMA((2, PARTS)),
+            pltpu.SemaphoreType.DMA((2,)),
         ],
-        compiler_params=PARAMS,
+        compiler_params=pltpu.CompilerParams(vmem_limit_bytes=61000 * 1024),
         cost_estimate=pl.CostEstimate(flops=1_000_000, bytes_accessed=800_000, transcendentals=0),
         name="gather",
     )(sources, targets)
@@ -200,21 +220,69 @@
 
 
 def from_behind(block):
-    wide, blk = lax.axis_size("wide"), lax.axis_size("blk")
-
-    def source(w, b):
-        return w * blk + b - 1 if b else (w - BLOCK) % wide * blk + blk - 1
-
-    route = [(source(w, b), w * blk + b) for w in range(wide) for b in range(blk)]
-    return lax.ppermute(block, ("wide", "blk"), route)
+    count = lax.axis_size("blk")
+    return lax.ppermute(block, "blk", [((i - 1) % count, i) for i in range(count)])
+
+
+def block_sum_body(came_ref, own_ref, *refs):
+    *out_refs, held = refs
+    total = came_ref[0].astype(jnp.float32)
+    for other in range(1, BLOCK):
+        total += came_ref[other].astype(jnp.float32)
+    held[...] = total
+    part = lax.div(lax.axis_index("wide"), BLOCK)
+    own_ref[...] = held[pl.ds(pl.multiple_of(part * TILES, TILES), TILES), :]
+    for ends, out_ref in zip(ROUNDS, out_refs, strict=True):
+        end = jnp.int32(0)
+        for start, chosen in ends.items():
+            end = jnp.where(part == start, chosen, end)
+        out_ref[...] = held[pl.ds(pl.multiple_of(end * TILES, TILES), TILES), :].astype(jnp.bfloat16)
+
+
+def block_sum(came):
+    shape = (TILES, LANES)
+    return pl.pallas_call(
+        block_sum_body,
+        out_shape=[jax.ShapeDtypeStruct(shape, jnp.float32)] + [jax.ShapeDtypeStruct(shape, jnp.bfloat16)] * len(ROUNDS),
+        in_specs=[VMEM],
+        out_specs=[VMEM] * (1 + len(ROUNDS)),
+        scratch_shapes=[pltpu.VMEM((PARTS * TILES, LANES), jnp.float32)],
+        compiler_params=PARAMS,
+        cost_estimate=pl.CostEstimate(flops=100_000, bytes_accessed=150_000, transcendentals=0),
+        name="block_sum",
+    )(came)
+
+
+def last_sum_body(own_ref, *refs):
+    total = own_ref[...]
+    for ref in refs[:-1]:
+        total += ref[...].astype(jnp.float32)
+    refs[-1][...] = total
+
+
+def last_sum(own, came):
+    return pl.pallas_call(
+        last_sum_body,
+        out_shape=jax.ShapeDtypeStruct((TILES, LANES), jnp.float32),
+        in_specs=[VMEM] * (1 + len(came)),
+        out_specs=VMEM,
+        compiler_params=PARAMS,
+        cost_estimate=pl.CostEstimate(flops=100_000, bytes_accessed=80_000, transcendentals=0),
+        name="last_sum",
+    )(own, *came)
 
 
 def shards(sources, targets):
     own = gathered(sources, targets)
     partial = exchange_term(own, from_behind(own))
-    arrived = lax.all_to_all(partial, "wide", split_axis=0, concat_axis=0, tiled=True)
-    summed = arrived.reshape(PIECES, -1, LANES).astype(jnp.float32).sum(axis=0)
-    return summed.reshape(1, -1)[:, :PIECE]
+    groups = [[part * BLOCK + i for i in range(BLOCK)] for part in range(PARTS)]
+    came = lax.all_to_all(partial, "wide", split_axis=0, concat_axis=0, axis_index_groups=groups, tiled=True)
+    mine, *sent = block_sum(came.reshape(BLOCK, PARTS * TILES, LANES))
+    arrived = []
+    for turn, ends in enumerate(ROUNDS):
+        route = [(start * BLOCK + i, end * BLOCK + i) for start, end in ends.items() for i in range(BLOCK)]
+        arrived.append(lax.ppermute(sent[turn], "wide", route))
+    return last_sum(mine, arrived).reshape(1, -1)[:, :PIECE]
 
 
 def solution(mesh):

time: 53.7 us -> 51.9 us (0.966)
  the two profiles are of different devices: /device:TPU:1 before, /device:TPU:384 now
where the time goes in v4:
time: 51.9 us; the launch traced here: 51.6 us
  waiting for transfers between devices  18.2 us (35%)
  starting transfers between devices  17.4 us (34%)
  blocking collectives  10.2 us (20%)
  Pallas kernels  5.24 us (10%)
    ppermute x7, starting transfers between devices, shards(): arrived.append(lax.ppermute(sent[turn], 'wide', route))  13.9 us
    all_to_all x1, blocking collectives, shards(): lax.all_to_all(partial, 'wide', split_axis=0, concat_axis=0, axis_index_g...  10.2 us
    ppermute x1, waiting for transfers between devices, from_behind(): lax.ppermute(block, 'blk', [((i - 1) % count, i) for i in range(count)])  10.1 us
    ppermute x7, waiting for transfers between devices, shards(): arrived.append(lax.ppermute(sent[turn], 'wide', route))  8.1 us
    ppermute x1, starting transfers between devices, from_behind(): lax.ppermute(block, 'blk', [((i - 1) % count, i) for i in range(count)])  3.48 us
    pallas_call x1, Pallas kernels, exchange_term(): pl.pallas_call(body, out_shape=jax.ShapeDtypeStruct((PIECES * TILES, LANE...  2.49 us
    pallas_call x1, Pallas kernels, gathered(): pl.pallas_call(gather_body, out_shape=jax.ShapeDtypeStruct((2 * PIECES, W...  2.11 us
  transfers between devices with their start and end apart: 8, of which 3 were waited for; matrix products, arithmetic and copies ran while one was open for 1% of the time, Pallas kernels for 0%

profile of v4, /device:TPU:384, one launch (start us, length us, event | category | flops | bytes accessed | tf_op | source)
XLA Modules:
  0.0 51.6 jit_solution(18237922218989578814)
XLA Ops:
  0.0 2.1 %gather.1.own_ref = bf16[64,2048]{1,0:T(8,128)(2,1)} custom-call(bf16[1,64000]{1,0:T(2,128)(2,1)} %s_ref.1, bf16[1,64000]{1,0:T(2,128)(2,1)} %t_ref.1), custom_call_target="tpu_custom_call" | custom-call | flops 1000000 | bytes 800000 | tf_op jit(solution)/shard_map/gather/pallas_call | solution.py:183
  2.1 3.5 %collective-permute-start = (bf16[64,2048]{1,0:T(8,128)(2,1)}, bf16[64,2048]{1,0:T(8,128)(2,1)S(1)}, u32[]{:S(2)}, u32[]{:S(2)}) collective-permute-start(bf16[64,2048]{1,0:T(8,128)(2,1)} %gather.1.own_ref), channel_id=1, source_target_pairs={{15,0},{0,1},{1,2},{2,3},{3,4},{4,5},{5,6},{6,7},{7,8},{8,9},{9,10... | collective-permute-start | bytes 786440 | tf_op jit(solution)/shard_map/ppermute | solution.py:224
  5.6 0.1 broadcast_add_fusion
  5.7 0.0 copy-start
  5.7 0.0 copy-start.1
  5.7 0.0 copy-start.2
  5.8 0.0 copy-start.3
  5.8 0.0 copy-start.4
  5.8 0.3 divide_multiply_fusion.kern_ref
  6.1 10.1 %collective-permute-done.came_ref = bf16[64,2048]{1,0:T(8,128)(2,1)S(1)} collective-permute-done((bf16[64,2048]{1,0:T(8,128)(2,1)}, bf16[64,2048]{1,0:T(8,128)(2,1)S(1)}, u32[]{:S(2)}, u32[]{:S(2)}) %collective-permute-start) | collective-permute-done | bytes 262176 | tf_op jit(solution)/shard_map/ppermute | solution.py:224
  16.2 0.0 copy-done
  16.2 0.0 copy-done.1
  16.2 0.0 copy-done.2
  16.2 0.0 copy-done.3
  16.2 0.0 copy-done.4
  16.2 2.5 %exchange.1 = bf16[512,128]{1,0:T(8,128)(2,1)S(1)} custom-call(bf16[64,2048]{1,0:T(8,128)(2,1)S(1)} %copy-done, bf16[64,2048]{1,0:T(8,128)(2,1)S(1)} %collective-permute-done.came_ref, f32[40,40,128]{2,1,0:T(8,128)S(1)} %divide_multiply_fusion.kern_ref, bf16[80,80]{1,0:T(8,128)(2,1)S(1)} %copy-done.4, bf16[80,80]{1,0:T(8,128)(2,1)S(1)} %copy-done.3, ...), custom_call_target="tpu_custom_call" | custom-call | flops 200000000 | bytes 2000000 | tf_op jit(solution)/shard_map/exchange/pallas_call | solution.py:204
  18.7 10.2 %all_to_all.9.came_ref = bf16[8,64,128]{2,1,0:T(8,128)(2,1)S(1)} all-to-all(bf16[8,64,128]{2,1,0:T(8,128)(2,1)S(1)} %bitcast.3), channel_id=1, replica_groups={{0,16,32,48,64,80,96,112},{128,144,160,176,192,208,224,240},{256,272,28..., dimensions={0} | all-to-all | bytes 262144 | tf_op jit(solution)/shard_map/all_to_all | solution.py:279
  28.9 0.7 %collective-permute-start.1 = (bf16[16,128]{1,0:T(8,128)(2,1)S(1)}, bf16[16,128]{1,0:T(8,128)(2,1)S(1)}, u32[]{:S(2)}, u32[]{:S(2)}) collective-permute-start(bf16[16,128]{1,0:T(8,128)(2,1)S(1)} %get-tuple-element.14), channel_id=1, source_target_pairs={{256,0},{272,16},{288,32},{304,48},{320,64},{336,80},{352,96},{368... | collective-permute-start | bytes 12296 | tf_op jit(solution)/shard_map/ppermute | solution.py:284
  29.6 1.3 %collective-permute-start.2 = (bf16[16,128]{1,0:T(8,128)(2,1)S(1)}, bf16[16,128]{1,0:T(8,128)(2,1)S(1)}, u32[]{:S(2)}, u32[]{:S(2)}) collective-permute-start(bf16[16,128]{1,0:T(8,128)(2,1)S(1)} %get-tuple-element.15), channel_id=1, source_target_pairs={{384,0},{400,16},{416,32},{432,48},{448,64},{464,80},{480,96},{496... | collective-permute-start | bytes 12296 | tf_op jit(solution)/shard_map/ppermute | solution.py:284
  30.9 4.5 %collective-permute-start.3 = (bf16[16,128]{1,0:T(8,128)(2,1)S(1)}, bf16[16,128]{1,0:T(8,128)(2,1)S(1)}, u32[]{:S(2)}, u32[]{:S(2)}) collective-permute-start(bf16[16,128]{1,0:T(8,128)(2,1)S(1)} %get-tuple-element.16), channel_id=1, source_target_pairs={{0,384},{16,400},{32,416},{48,432},{64,448},{80,464},{96,480},{112... | collective-permute-start | bytes 12296 | tf_op jit(solution)/shard_map/ppermute | solution.py:284
  35.4 0.7 %collective-permute-start.4 = (bf16[16,128]{1,0:T(8,128)(2,1)S(1)}, bf16[16,128]{1,0:T(8,128)(2,1)S(1)}, u32[]{:S(2)}, u32[]{:S(2)}) collective-permute-start(bf16[16,128]{1,0:T(8,128)(2,1)S(1)} %get-tuple-element.17), channel_id=1, source_target_pairs={{0,128},{16,144},{32,160},{48,176},{64,192},{80,208},{96,224},{112... | collective-permute-start | bytes 12296 | tf_op jit(solution)/shard_map/ppermute | solution.py:284
  36.0 1.3 %collective-permute-start.5 = (bf16[16,128]{1,0:T(8,128)(2,1)S(1)}, bf16[16,128]{1,0:T(8,128)(2,1)S(1)}, u32[]{:S(2)}, u32[]{:S(2)}) collective-permute-start(bf16[16,128]{1,0:T(8,128)(2,1)S(1)} %get-tuple-element.18), channel_id=1, source_target_pairs={{0,256},{16,272},{32,288},{48,304},{64,320},{80,336},{96,352},{112... | collective-permute-start | bytes 12296 | tf_op jit(solution)/shard_map/ppermute | solution.py:284
  37.3 0.0 collective-permute-done.1.refs_0_
  37.3 4.2 %collective-permute-start.6 = (bf16[16,128]{1,0:T(8,128)(2,1)S(1)}, bf16[16,128]{1,0:T(8,128)(2,1)S(1)}, u32[]{:S(2)}, u32[]{:S(2)}) collective-permute-start(bf16[16,128]{1,0:T(8,128)(2,1)S(1)} %get-tuple-element.19), channel_id=1, source_target_pairs={{384,256},{400,272},{416,288},{432,304},{448,320},{464,336},{480,3... | collective-permute-start | bytes 12296 | tf_op jit(solution)/shard_map/ppermute | solution.py:284
  41.6 0.0 collective-permute-done.2.refs_1_
  41.6 1.3 %collective-permute-start.7 = (bf16[16,128]{1,0:T(8,128)(2,1)S(1)}, bf16[16,128]{1,0:T(8,128)(2,1)S(1)}, u32[]{:S(2)}, u32[]{:S(2)}) collective-permute-start(bf16[16,128]{1,0:T(8,128)(2,1)S(1)} %get-tuple-element.20), channel_id=1, source_target_pairs={{128,256},{144,272},{160,288},{176,304},{192,320},{208,336},{224,3... | collective-permute-start | bytes 12296 | tf_op jit(solution)/shard_map/ppermute | solution.py:284
  42.9 0.0 collective-permute-done.3.refs_2_
  42.9 0.0 collective-permute-done.4.refs_3_
  42.9 7.3 %collective-permute-done.5.refs_4_ = bf16[16,128]{1,0:T(8,128)(2,1)S(1)} collective-permute-done((bf16[16,128]{1,0:T(8,128)(2,1)S(1)}, bf16[16,128]{1,0:T(8,128)(2,1)S(1)}, u32[]{:S(2)}, u32[]{:S(2)}) %collective-permute-start.5) | collective-permute-done | bytes 4128 | tf_op jit(solution)/shard_map/ppermute | solution.py:284
  50.2 0.0 collective-permute-done.6.refs_5_
  50.2 0.8 %collective-permute-done.7.refs_6_ = bf16[16,128]{1,0:T(8,128)(2,1)S(1)} collective-permute-done((bf16[16,128]{1,0:T(8,128)(2,1)S(1)}, bf16[16,128]{1,0:T(8,128)(2,1)S(1)}, u32[]{:S(2)}, u32[]{:S(2)}) %collective-permute-start.7) | collective-permute-done | bytes 4128 | tf_op jit(solution)/shard_map/ppermute | solution.py:284
  51.0 0.6 %last_sum.1 = f32[16,128]{1,0:T(8,128)} custom-call(f32[16,128]{1,0:T(8,128)S(1)} %get-tuple-element.13.own_ref, bf16[16,128]{1,0:T(8,128)(2,1)S(1)} %collective-permute-done.1.refs_0_, bf16[16,128]{1,0:T(8,128)(2,1)S(1)} %collective-permute-done.2.refs_1_, bf16[16,128]{1,0:T(8,128)(2,1)S(1)} %collective-permute-done.3.refs_2_, ...), custom_call_target="tpu_custom_call" | custom-call | flops 100000 | bytes 80000 | tf_op jit(solution)/shard_map/last_sum/pallas_call | solution.py:264
  (3 shorter events, 0.1 us)
Async XLA Ops:
  2.1 14.1 %collective-permute-start = (bf16[64,2048]{1,0:T(8,128)(2,1)}, bf16[64,2048]{1,0:T(8,128)(2,1)S(1)}, u32[]{:S(2)}, u32[]{:S(2)}) collective-permute-start(bf16[64,2048]{1,0:T(8,128)(2,1)} %gather.1.own_ref), channel_id=1, source_target_pairs={{15,0},{0,1},{1,2},{2,3},{3,4},{4,5},{5,6},{6,7},{7,8},{8,9},{9,10... | collective-permute-start | bytes 786440 | tf_op jit(solution)/shard_map/ppermute | solution.py:224
  5.7 10.5 %copy-start = (bf16[64,2048]{1,0:T(8,128)(2,1)S(1)}, bf16[64,2048]{1,0:T(8,128)(2,1)}, u32[]{:S(2)}) copy-start(bf16[64,2048]{1,0:T(8,128)(2,1)} %gather.1.own_ref) | copy-start | bytes 786436
  5.7 10.4 %copy-start.1 = (bf16[256,128]{1,0:T(8,128)(2,1)S(1)}, bf16[256,128]{1,0:T(8,128)(2,1)}, u32[]{:S(2)}) copy-start(bf16[256,128]{1,0:T(8,128)(2,1)} %constant.48.clone.last_ref) | copy-start | bytes 196612
  5.7 10.4 %copy-start.2 = (bf16[128,256]{1,0:T(8,128)(2,1)S(1)}, bf16[128,256]{1,0:T(8,128)(2,1)}, u32[]{:S(2)}) copy-start(bf16[128,256]{1,0:T(8,128)(2,1)} %constant.47.clone.first_ref) | copy-start | bytes 196612
  5.8 10.4 %copy-start.3 = (bf16[80,80]{1,0:T(8,128)(2,1)S(1)}, bf16[80,80]{1,0:T(8,128)(2,1)}, u32[]{:S(2)}) copy-start(bf16[80,80]{1,0:T(8,128)(2,1)} %constant.46.clone.inv_ref) | copy-start | bytes 38404
  5.8 10.4 %copy-start.4 = (bf16[80,80]{1,0:T(8,128)(2,1)S(1)}, bf16[80,80]{1,0:T(8,128)(2,1)}, u32[]{:S(2)}) copy-start(bf16[80,80]{1,0:T(8,128)(2,1)} %constant.45.clone.fwd_ref) | copy-start | bytes 38404
  28.9 8.4 %collective-permute-start.1 = (bf16[16,128]{1,0:T(8,128)(2,1)S(1)}, bf16[16,128]{1,0:T(8,128)(2,1)S(1)}, u32[]{:S(2)}, u32[]{:S(2)}) collective-permute-start(bf16[16,128]{1,0:T(8,128)(2,1)S(1)} %get-tuple-element.14), channel_id=1, source_target_pairs={{256,0},{272,16},{288,32},{304,48},{320,64},{336,80},{352,96},{368... | collective-permute-start | bytes 12296 | tf_op jit(solution)/shard_map/ppermute | solution.py:284
  29.6 12.0 %collective-permute-start.2 = (bf16[16,128]{1,0:T(8,128)(2,1)S(1)}, bf16[16,128]{1,0:T(8,128)(2,1)S(1)}, u32[]{:S(2)}, u32[]{:S(2)}) collective-permute-start(bf16[16,128]{1,0:T(8,128)(2,1)S(1)} %get-tuple-element.15), channel_id=1, source_target_pairs={{384,0},{400,16},{416,32},{432,48},{448,64},{464,80},{480,96},{496... | collective-permute-start | bytes 12296 | tf_op jit(solution)/shard_map/ppermute | solution.py:284
  30.9 12.0 %collective-permute-start.3 = (bf16[16,128]{1,0:T(8,128)(2,1)S(1)}, bf16[16,128]{1,0:T(8,128)(2,1)S(1)}, u32[]{:S(2)}, u32[]{:S(2)}) collective-permute-start(bf16[16,128]{1,0:T(8,128)(2,1)S(1)} %get-tuple-element.16), channel_id=1, source_target_pairs={{0,384},{16,400},{32,416},{48,432},{64,448},{80,464},{96,480},{112... | collective-permute-start | bytes 12296 | tf_op jit(solution)/shard_map/ppermute | solution.py:284
  35.4 7.5 %collective-permute-start.4 = (bf16[16,128]{1,0:T(8,128)(2,1)S(1)}, bf16[16,128]{1,0:T(8,128)(2,1)S(1)}, u32[]{:S(2)}, u32[]{:S(2)}) collective-permute-start(bf16[16,128]{1,0:T(8,128)(2,1)S(1)} %get-tuple-element.17), channel_id=1, source_target_pairs={{0,128},{16,144},{32,160},{48,176},{64,192},{80,208},{96,224},{112... | collective-permute-start | bytes 12296 | tf_op jit(solution)/shard_map/ppermute | solution.py:284
  36.0 14.2 %collective-permute-start.5 = (bf16[16,128]{1,0:T(8,128)(2,1)S(1)}, bf16[16,128]{1,0:T(8,128)(2,1)S(1)}, u32[]{:S(2)}, u32[]{:S(2)}) collective-permute-start(bf16[16,128]{1,0:T(8,128)(2,1)S(1)} %get-tuple-element.18), channel_id=1, source_target_pairs={{0,256},{16,272},{32,288},{48,304},{64,320},{80,336},{96,352},{112... | collective-permute-start | bytes 12296 | tf_op jit(solution)/shard_map/ppermute | solution.py:284
  37.3 12.9 %collective-permute-start.6 = (bf16[16,128]{1,0:T(8,128)(2,1)S(1)}, bf16[16,128]{1,0:T(8,128)(2,1)S(1)}, u32[]{:S(2)}, u32[]{:S(2)}) collective-permute-start(bf16[16,128]{1,0:T(8,128)(2,1)S(1)} %get-tuple-element.19), channel_id=1, source_target_pairs={{384,256},{400,272},{416,288},{432,304},{448,320},{464,336},{480,3... | collective-permute-start | bytes 12296 | tf_op jit(solution)/shard_map/ppermute | solution.py:284
  41.6 9.4 %collective-permute-start.7 = (bf16[16,128]{1,0:T(8,128)(2,1)S(1)}, bf16[16,128]{1,0:T(8,128)(2,1)S(1)}, u32[]{:S(2)}, u32[]{:S(2)}) collective-permute-start(bf16[16,128]{1,0:T(8,128)(2,1)S(1)} %get-tuple-element.20), channel_id=1, source_target_pairs={{128,256},{144,272},{160,288},{176,304},{192,320},{208,336},{224,3... | collective-permute-start | bytes 12296 | tf_op jit(solution)/shard_map/ppermute | solution.py:284

commit v5 on v4

--- a/solution.py
+++ b/solution.py
@@ -21,6 +21,7 @@
 FLAT = GRID**3 // LANES
 CYCLE = 8
 PARTS = 4
+STEPS = 2
 ROUNDS = ({2: 0}, {3: 0}, {0: 3, 1: 0, 3: 1}, {0: 1}, {0: 2, 1: 3, 2: 1}, {3: 2}, {1: 2, 2: 3})
 BLOCK = 8
 SCREEN = 0.3
@@ -43,12 +44,15 @@
     def left(sign):
         return np.block([[cos, sign * sin], [-sign * sin, cos]])
 
-    spread = np.zeros((2 * LANES, LANES), np.float32)
-    first = np.zeros((LANES, 2 * LANES), np.float32)
-    for row, col, table in ((0, 0, cos), (0, 1, -sin), (1, 0, sin), (1, 1, cos)):
-        first[row * HALF : row * HALF + GRID, col * LANES : col * LANES + GRID] = table
-    for row, col, table in ((0, 0, cos), (0, 1, sin), (1, 0, -sin), (1, 1, cos)):
-        spread[row * LANES : row * LANES + GRID, col * HALF : col * HALF + GRID] = table
+    first = np.zeros((2 * LANES, 2 * LANES), np.float32)
+    spread = np.zeros((2 * LANES, 2 * LANES), np.float32)
+    for plane in range(2):
+        for row, col, cosine, sine in ((0, 0, cos, 0.0), (0, 1, 0.0, -sin), (1, 0, 0.0, sin), (1, 1, cos, 0.0)):
+            near, far = plane * LANES + row * HALF, col * LANES + plane * HALF
+            first[near : near + GRID, far : far + GRID] = cosine + sine
+        for row, col, cosine, sine in ((0, 0, cos, 0.0), (0, 1, 0.0, sin), (1, 0, 0.0, -sin), (1, 1, cos, 0.0)):
+            near, far = row * LANES + plane * HALF, plane * LANES + col * HALF
+            spread[near : near + GRID, far : far + GRID] = cosine + sine
     return left(1.0), left(-1.0), first, spread
 
 
@@ -96,7 +100,7 @@
         copy.wait()
 
 
-def body(own_ref, came_ref, kern_ref, fwd_ref, inv_ref, first_ref, last_ref, out_ref, xs, real, imag, flat, sums):
+def body(own_ref, came_ref, kern_ref, fwd_ref, inv_ref, first_ref, last_ref, out_ref, xs, near, real, imag, real_back, imag_back, back, ys, flat, sums):
     lane = lax.broadcasted_iota(jnp.int32, (PIECES, LANES), 1)
     low = lane < HALF
 
@@ -128,37 +132,60 @@
     def stacked(rows):
         return jnp.concatenate([real[rows, :], imag[rows, :]], axis=0)
 
-    def put(rows, value):
-        real[rows, :] = value[:GRID]
-        imag[rows, :] = value[GRID:]
-
-    def along_b(table):
-        for pair in range(GRID // 2):
-            one, two = pl.ds(2 * pair * GRID, GRID), pl.ds((2 * pair + 1) * GRID, GRID)
-            value = turned(table, stacked(one), stacked(two))
-            put(one, value[:, re])
-            put(two, value[:, im])
-
-    spread = jnp.dot(xs[...].astype(jnp.bfloat16), first_ref[...], preferred_element_type=jnp.float32)
-    real[...] = spread[:, re]
-    imag[...] = spread[:, im]
-    along_b(forward)
+    def put(refs, rows, value):
+        refs[0][rows, :] = value[:GRID]
+        refs[1][rows, :] = value[GRID:]
+
+    def plane(index):
+        return pl.ds(index * GRID, GRID)
+
+    def paired(index):
+        rows, far = plane(index), plane(index + GRID // 2)
+        both = [jnp.where(low_rows, ref[rows, :], pltpu.roll(ref[far, :], HALF, 1)) for ref in (real_back, imag_back)]
+        return jnp.concatenate(both, axis=0)
+
+    low_rows = lax.broadcasted_iota(jnp.int32, (GRID, LANES), 1) < HALF
+
+    def along_c(source, table_ref, result, step):
+        size = ROWS // 2 // STEPS
+        one, two = pl.ds(step * size, size), pl.ds(ROWS // 2 + step * size, size)
+        both = jnp.concatenate([source[one, :], source[two, :]], axis=1).astype(jnp.bfloat16)
+        value = jnp.dot(both, table_ref[...], preferred_element_type=jnp.float32)
+        result[one, :] = value[:, re]
+        result[two, :] = value[:, im]
+
+    pairs = GRID // 4 // STEPS
+    for step in range(STEPS):
+        along_c(xs, first_ref, near, step)
+    for step in range(STEPS):
+        for pair in range(step * pairs, (step + 1) * pairs):
+            chosen = (2 * pair, 2 * pair + 1)
+            slabs = [jnp.concatenate([near[plane(index), :], near[plane(index + GRID // 2), :]], axis=0) for index in chosen]
+            value = turned(forward, *slabs)
+            for index, part in zip(chosen, (re, im), strict=True):
+                put((real, imag), plane(index), value[:, part])
+                put((real, imag), plane(index + GRID // 2), pltpu.roll(value[:, part], HALF, 1))
     for pair in range(GRID // 2):
         one, two = pl.ds(2 * pair, GRID, stride=GRID), pl.ds(2 * pair + 1, GRID, stride=GRID)
         value = turned(forward, stacked(one), stacked(two))
         scale = [jnp.concatenate([kern_ref[2 * pair + which]] * 2, axis=0) for which in range(2)]
         value = turned(inverse, value[:, re] * scale[0], value[:, im] * scale[1])
-        put(one, value[:, re])
-        put(two, value[:, im])
-    along_b(inverse)
-    both = jnp.concatenate([real[...], imag[...]], axis=1).astype(jnp.bfloat16)
-    xs[...] = jnp.dot(both, last_ref[...], preferred_element_type=jnp.float32)
+        put((real_back, imag_back), one, value[:, re])
+        put((real_back, imag_back), two, value[:, im])
+    for step in range(STEPS):
+        for pair in range(step * pairs, (step + 1) * pairs):
+            value = turned(inverse, paired(2 * pair), paired(2 * pair + 1))
+            for index, part in ((2 * pair, re), (2 * pair + 1, im)):
+                back[plane(index), :] = value[:GRID, part]
+                back[plane(index + GRID // 2), :] = value[GRID:, part]
+    for step in range(STEPS):
+        along_c(back, last_ref, ys, step)
 
     tiles = [[None] * TILES for _ in range(2)]
     for group in range(GROUPS):
         start = GRID * group
         tile, shift = start // LANES, start % LANES
-        value = xs[pl.ds(group, PIECES, stride=GROUPS), :].astype(jnp.bfloat16)
+        value = ys[pl.ds(group, PIECES, stride=GROUPS), :].astype(jnp.bfloat16)
         for which in range(2):
             turn = (shift - HALF * which) % LANES
             moved = pltpu.roll(value, turn, 1) if turn else value
@@ -207,9 +234,7 @@
         in_specs=[VMEM] * 7,
         out_specs=VMEM,
         scratch_shapes=[
-            pltpu.VMEM((ROWS, LANES), jnp.float32),
-            pltpu.VMEM((ROWS, LANES), jnp.float32),
-            pltpu.VMEM((ROWS, LANES), jnp.float32),
+            *[pltpu.VMEM((ROWS, LANES), jnp.float32)] * 8,
             pltpu.VMEM((2, PIECES, WIDE), jnp.bfloat16),
             pltpu.VMEM((PIECES * TILES, LANES), jnp.float32),
         ],

time: 51.9 us -> 51.8 us (level)
  no operation moved by 1% of the time
where the time goes in v5:
time: 51.8 us; the launch traced here: 51.5 us
  waiting for transfers between devices  18.2 us (35%)
  starting transfers between devices  17.4 us (34%)
  blocking collectives  10.2 us (20%)
  Pallas kernels  5.1 us (10%)
    ppermute x7, starting transfers between devices, shards(): arrived.append(lax.ppermute(sent[turn], 'wide', route))  13.9 us
    all_to_all x1, blocking collectives, shards(): lax.all_to_all(partial, 'wide', split_axis=0, concat_axis=0, axis_index_g...  10.2 us
    ppermute x1, waiting for transfers between devices, from_behind(): lax.ppermute(block, 'blk', [((i - 1) % count, i) for i in range(count)])  10.1 us
    ppermute x7, waiting for transfers between devices, shards(): arrived.append(lax.ppermute(sent[turn], 'wide', route))  8.1 us
    ppermute x1, starting transfers between devices, from_behind(): lax.ppermute(block, 'blk', [((i - 1) % count, i) for i in range(count)])  3.48 us
    pallas_call x1, Pallas kernels, exchange_term(): pl.pallas_call(body, out_shape=jax.ShapeDtypeStruct((PIECES * TILES, LANE...  2.36 us
    pallas_call x1, Pallas kernels, gathered(): pl.pallas_call(gather_body, out_shape=jax.ShapeDtypeStruct((2 * PIECES, W...  2.11 us
  transfers between devices with their start and end apart: 8, of which 3 were waited for; matrix products, arithmetic and copies ran while one was open for 1% of the time, Pallas kernels for 0%

profile of v5, /device:TPU:384, one launch (start us, length us, event | category | flops | bytes accessed | tf_op | source)
XLA Modules:
  0.0 51.5 jit_solution(10876572031186820819)
XLA Ops:
  0.0 2.1 %gather.1.own_ref = bf16[64,2048]{1,0:T(8,128)(2,1)} custom-call(bf16[1,64000]{1,0:T(2,128)(2,1)} %s_ref.1, bf16[1,64000]{1,0:T(2,128)(2,1)} %t_ref.1), custom_call_target="tpu_custom_call" | custom-call | flops 1000000 | bytes 800000 | tf_op jit(solution)/shard_map/gather/pallas_call | solution.py:210
  2.1 3.5 %collective-permute-start = (bf16[64,2048]{1,0:T(8,128)(2,1)}, bf16[64,2048]{1,0:T(8,128)(2,1)S(1)}, u32[]{:S(2)}, u32[]{:S(2)}) collective-permute-start(bf16[64,2048]{1,0:T(8,128)(2,1)} %gather.1.own_ref), channel_id=1, source_target_pairs={{15,0},{0,1},{1,2},{2,3},{3,4},{4,5},{5,6},{6,7},{7,8},{8,9},{9,10... | collective-permute-start | bytes 786440 | tf_op jit(solution)/shard_map/ppermute | solution.py:249
  5.6 0.1 broadcast_add_fusion
  5.7 0.0 copy-start
  5.7 0.0 copy-start.1
  5.7 0.0 copy-start.2
  5.8 0.0 copy-start.3
  5.8 0.0 copy-start.4
  5.8 0.3 divide_multiply_fusion.kern_ref
  6.1 10.1 %collective-permute-done.came_ref = bf16[64,2048]{1,0:T(8,128)(2,1)S(1)} collective-permute-done((bf16[64,2048]{1,0:T(8,128)(2,1)}, bf16[64,2048]{1,0:T(8,128)(2,1)S(1)}, u32[]{:S(2)}, u32[]{:S(2)}) %collective-permute-start) | collective-permute-done | bytes 262176 | tf_op jit(solution)/shard_map/ppermute | solution.py:249
  16.2 0.0 copy-done
  16.2 0.0 copy-done.1
  16.2 0.0 copy-done.2
  16.2 0.0 copy-done.3
  16.2 0.0 copy-done.4
  16.2 2.4 %exchange.1 = bf16[512,128]{1,0:T(8,128)(2,1)S(1)} custom-call(bf16[64,2048]{1,0:T(8,128)(2,1)S(1)} %copy-done, bf16[64,2048]{1,0:T(8,128)(2,1)S(1)} %collective-permute-done.came_ref, f32[40,40,128]{2,1,0:T(8,128)S(1)} %divide_multiply_fusion.kern_ref, bf16[80,80]{1,0:T(8,128)(2,1)S(1)} %copy-done.4, bf16[80,80]{1,0:T(8,128)(2,1)S(1)} %copy-done.3, ...), custom_call_target="tpu_custom_call" | custom-call | flops 200000000 | bytes 2000000 | tf_op jit(solution)/shard_map/exchange/pallas_call | solution.py:231
  18.6 10.2 %all_to_all.9.came_ref = bf16[8,64,128]{2,1,0:T(8,128)(2,1)S(1)} all-to-all(bf16[8,64,128]{2,1,0:T(8,128)(2,1)S(1)} %bitcast.3), channel_id=1, replica_groups={{0,16,32,48,64,80,96,112},{128,144,160,176,192,208,224,240},{256,272,28..., dimensions={0} | all-to-all | bytes 262144 | tf_op jit(solution)/shard_map/all_to_all | solution.py:304
  28.8 0.7 %collective-permute-start.1 = (bf16[16,128]{1,0:T(8,128)(2,1)S(1)}, bf16[16,128]{1,0:T(8,128)(2,1)S(1)}, u32[]{:S(2)}, u32[]{:S(2)}) collective-permute-start(bf16[16,128]{1,0:T(8,128)(2,1)S(1)} %get-tuple-element.14), channel_id=1, source_target_pairs={{256,0},{272,16},{288,32},{304,48},{320,64},{336,80},{352,96},{368... | collective-permute-start | bytes 12296 | tf_op jit(solution)/shard_map/ppermute | solution.py:309
  29.5 1.3 %collective-permute-start.2 = (bf16[16,128]{1,0:T(8,128)(2,1)S(1)}, bf16[16,128]{1,0:T(8,128)(2,1)S(1)}, u32[]{:S(2)}, u32[]{:S(2)}) collective-permute-start(bf16[16,128]{1,0:T(8,128)(2,1)S(1)} %get-tuple-element.15), channel_id=1, source_target_pairs={{384,0},{400,16},{416,32},{432,48},{448,64},{464,80},{480,96},{496... | collective-permute-start | bytes 12296 | tf_op jit(solution)/shard_map/ppermute | solution.py:309
  30.8 4.4 %collective-permute-start.3 = (bf16[16,128]{1,0:T(8,128)(2,1)S(1)}, bf16[16,128]{1,0:T(8,128)(2,1)S(1)}, u32[]{:S(2)}, u32[]{:S(2)}) collective-permute-start(bf16[16,128]{1,0:T(8,128)(2,1)S(1)} %get-tuple-element.16), channel_id=1, source_target_pairs={{0,384},{16,400},{32,416},{48,432},{64,448},{80,464},{96,480},{112... | collective-permute-start | bytes 12296 | tf_op jit(solution)/shard_map/ppermute | solution.py:309
  35.2 0.7 %collective-permute-start.4 = (bf16[16,128]{1,0:T(8,128)(2,1)S(1)}, bf16[16,128]{1,0:T(8,128)(2,1)S(1)}, u32[]{:S(2)}, u32[]{:S(2)}) collective-permute-start(bf16[16,128]{1,0:T(8,128)(2,1)S(1)} %get-tuple-element.17), channel_id=1, source_target_pairs={{0,128},{16,144},{32,160},{48,176},{64,192},{80,208},{96,224},{112... | collective-permute-start | bytes 12296 | tf_op jit(solution)/shard_map/ppermute | solution.py:309
  35.9 1.3 %collective-permute-start.5 = (bf16[16,128]{1,0:T(8,128)(2,1)S(1)}, bf16[16,128]{1,0:T(8,128)(2,1)S(1)}, u32[]{:S(2)}, u32[]{:S(2)}) collective-permute-start(bf16[16,128]{1,0:T(8,128)(2,1)S(1)} %get-tuple-element.18), channel_id=1, source_target_pairs={{0,256},{16,272},{32,288},{48,304},{64,320},{80,336},{96,352},{112... | collective-permute-start | bytes 12296 | tf_op jit(solution)/shard_map/ppermute | solution.py:309
  37.2 0.0 collective-permute-done.1.refs_0_
  37.2 4.2 %collective-permute-start.6 = (bf16[16,128]{1,0:T(8,128)(2,1)S(1)}, bf16[16,128]{1,0:T(8,128)(2,1)S(1)}, u32[]{:S(2)}, u32[]{:S(2)}) collective-permute-start(bf16[16,128]{1,0:T(8,128)(2,1)S(1)} %get-tuple-element.19), channel_id=1, source_target_pairs={{384,256},{400,272},{416,288},{432,304},{448,320},{464,336},{480,3... | collective-permute-start | bytes 12296 | tf_op jit(solution)/shard_map/ppermute | solution.py:309
  41.5 0.0 collective-permute-done.2.refs_1_
  41.5 1.3 %collective-permute-start.7 = (bf16[16,128]{1,0:T(8,128)(2,1)S(1)}, bf16[16,128]{1,0:T(8,128)(2,1)S(1)}, u32[]{:S(2)}, u32[]{:S(2)}) collective-permute-start(bf16[16,128]{1,0:T(8,128)(2,1)S(1)} %get-tuple-element.20), channel_id=1, source_target_pairs={{128,256},{144,272},{160,288},{176,304},{192,320},{208,336},{224,3... | collective-permute-start | bytes 12296 | tf_op jit(solution)/shard_map/ppermute | solution.py:309
  42.8 0.0 collective-permute-done.3.refs_2_
  42.8 0.0 collective-permute-done.4.refs_3_
  42.8 7.3 %collective-permute-done.5.refs_4_ = bf16[16,128]{1,0:T(8,128)(2,1)S(1)} collective-permute-done((bf16[16,128]{1,0:T(8,128)(2,1)S(1)}, bf16[16,128]{1,0:T(8,128)(2,1)S(1)}, u32[]{:S(2)}, u32[]{:S(2)}) %collective-permute-start.5) | collective-permute-done | bytes 4128 | tf_op jit(solution)/shard_map/ppermute | solution.py:309
  50.1 0.0 collective-permute-done.6.refs_5_
  50.1 0.8 %collective-permute-done.7.refs_6_ = bf16[16,128]{1,0:T(8,128)(2,1)S(1)} collective-permute-done((bf16[16,128]{1,0:T(8,128)(2,1)S(1)}, bf16[16,128]{1,0:T(8,128)(2,1)S(1)}, u32[]{:S(2)}, u32[]{:S(2)}) %collective-permute-start.7) | collective-permute-done | bytes 4128 | tf_op jit(solution)/shard_map/ppermute | solution.py:309
  50.9 0.6 %last_sum.1 = f32[16,128]{1,0:T(8,128)} custom-call(f32[16,128]{1,0:T(8,128)S(1)} %get-tuple-element.13.own_ref, bf16[16,128]{1,0:T(8,128)(2,1)S(1)} %collective-permute-done.1.refs_0_, bf16[16,128]{1,0:T(8,128)(2,1)S(1)} %collective-permute-done.2.refs_1_, bf16[16,128]{1,0:T(8,128)(2,1)S(1)} %collective-permute-done.3.refs_2_, ...), custom_call_target="tpu_custom_call" | custom-call | flops 100000 | bytes 80000 | tf_op jit(solution)/shard_map/last_sum/pallas_call | solution.py:289
  (3 shorter events, 0.1 us)
Async XLA Ops:
  2.1 14.1 %collective-permute-start = (bf16[64,2048]{1,0:T(8,128)(2,1)}, bf16[64,2048]{1,0:T(8,128)(2,1)S(1)}, u32[]{:S(2)}, u32[]{:S(2)}) collective-permute-start(bf16[64,2048]{1,0:T(8,128)(2,1)} %gather.1.own_ref), channel_id=1, source_target_pairs={{15,0},{0,1},{1,2},{2,3},{3,4},{4,5},{5,6},{6,7},{7,8},{8,9},{9,10... | collective-permute-start | bytes 786440 | tf_op jit(solution)/shard_map/ppermute | solution.py:249
  5.7 10.5 %copy-start = (bf16[64,2048]{1,0:T(8,128)(2,1)S(1)}, bf16[64,2048]{1,0:T(8,128)(2,1)}, u32[]{:S(2)}) copy-start(bf16[64,2048]{1,0:T(8,128)(2,1)} %gather.1.own_ref) | copy-start | bytes 786436
  5.7 10.4 %copy-start.1 = (bf16[256,256]{1,0:T(8,128)(2,1)S(1)}, bf16[256,256]{1,0:T(8,128)(2,1)}, u32[]{:S(2)}) copy-start(bf16[256,256]{1,0:T(8,128)(2,1)} %constant.48.clone.last_ref) | copy-start | bytes 393220
  5.7 10.4 %copy-start.2 = (bf16[256,256]{1,0:T(8,128)(2,1)S(1)}, bf16[256,256]{1,0:T(8,128)(2,1)}, u32[]{:S(2)}) copy-start(bf16[256,256]{1,0:T(8,128)(2,1)} %constant.47.clone.first_ref) | copy-start | bytes 393220
  5.8 10.4 %copy-start.3 = (bf16[80,80]{1,0:T(8,128)(2,1)S(1)}, bf16[80,80]{1,0:T(8,128)(2,1)}, u32[]{:S(2)}) copy-start(bf16[80,80]{1,0:T(8,128)(2,1)} %constant.46.clone.inv_ref) | copy-start | bytes 38404
  5.8 10.4 %copy-start.4 = (bf16[80,80]{1,0:T(8,128)(2,1)S(1)}, bf16[80,80]{1,0:T(8,128)(2,1)}, u32[]{:S(2)}) copy-start(bf16[80,80]{1,0:T(8,128)(2,1)} %constant.45.clone.fwd_ref) | copy-start | bytes 38404
  28.8 8.4 %collective-permute-start.1 = (bf16[16,128]{1,0:T(8,128)(2,1)S(1)}, bf16[16,128]{1,0:T(8,128)(2,1)S(1)}, u32[]{:S(2)}, u32[]{:S(2)}) collective-permute-start(bf16[16,128]{1,0:T(8,128)(2,1)S(1)} %get-tuple-element.14), channel_id=1, source_target_pairs={{256,0},{272,16},{288,32},{304,48},{320,64},{336,80},{352,96},{368... | collective-permute-start | bytes 12296 | tf_op jit(solution)/shard_map/ppermute | solution.py:309
  29.5 12.0 %collective-permute-start.2 = (bf16[16,128]{1,0:T(8,128)(2,1)S(1)}, bf16[16,128]{1,0:T(8,128)(2,1)S(1)}, u32[]{:S(2)}, u32[]{:S(2)}) collective-permute-start(bf16[16,128]{1,0:T(8,128)(2,1)S(1)} %get-tuple-element.15), channel_id=1, source_target_pairs={{384,0},{400,16},{416,32},{432,48},{448,64},{464,80},{480,96},{496... | collective-permute-start | bytes 12296 | tf_op jit(solution)/shard_map/ppermute | solution.py:309
  30.8 12.0 %collective-permute-start.3 = (bf16[16,128]{1,0:T(8,128)(2,1)S(1)}, bf16[16,128]{1,0:T(8,128)(2,1)S(1)}, u32[]{:S(2)}, u32[]{:S(2)}) collective-permute-start(bf16[16,128]{1,0:T(8,128)(2,1)S(1)} %get-tuple-element.16), channel_id=1, source_target_pairs={{0,384},{16,400},{32,416},{48,432},{64,448},{80,464},{96,480},{112... | collective-permute-start | bytes 12296 | tf_op jit(solution)/shard_map/ppermute | solution.py:309
  35.2 7.6 %collective-permute-start.4 = (bf16[16,128]{1,0:T(8,128)(2,1)S(1)}, bf16[16,128]{1,0:T(8,128)(2,1)S(1)}, u32[]{:S(2)}, u32[]{:S(2)}) collective-permute-start(bf16[16,128]{1,0:T(8,128)(2,1)S(1)} %get-tuple-element.17), channel_id=1, source_target_pairs={{0,128},{16,144},{32,160},{48,176},{64,192},{80,208},{96,224},{112... | collective-permute-start | bytes 12296 | tf_op jit(solution)/shard_map/ppermute | solution.py:309
  35.9 14.2 %collective-permute-start.5 = (bf16[16,128]{1,0:T(8,128)(2,1)S(1)}, bf16[16,128]{1,0:T(8,128)(2,1)S(1)}, u32[]{:S(2)}, u32[]{:S(2)}) collective-permute-start(bf16[16,128]{1,0:T(8,128)(2,1)S(1)} %get-tuple-element.18), channel_id=1, source_target_pairs={{0,256},{16,272},{32,288},{48,304},{64,320},{80,336},{96,352},{112... | collective-permute-start | bytes 12296 | tf_op jit(solution)/shard_map/ppermute | solution.py:309
  37.2 12.9 %collective-permute-start.6 = (bf16[16,128]{1,0:T(8,128)(2,1)S(1)}, bf16[16,128]{1,0:T(8,128)(2,1)S(1)}, u32[]{:S(2)}, u32[]{:S(2)}) collective-permute-start(bf16[16,128]{1,0:T(8,128)(2,1)S(1)} %get-tuple-element.19), channel_id=1, source_target_pairs={{384,256},{400,272},{416,288},{432,304},{448,320},{464,336},{480,3... | collective-permute-start | bytes 12296 | tf_op jit(solution)/shard_map/ppermute | solution.py:309
  41.5 9.4 %collective-permute-start.7 = (bf16[16,128]{1,0:T(8,128)(2,1)S(1)}, bf16[16,128]{1,0:T(8,128)(2,1)S(1)}, u32[]{:S(2)}, u32[]{:S(2)}) collective-permute-start(bf16[16,128]{1,0:T(8,128)(2,1)S(1)} %get-tuple-element.20), channel_id=1, source_target_pairs={{128,256},{144,272},{160,288},{176,304},{192,320},{208,336},{224,3... | collective-permute-start | bytes 12296 | tf_op jit(solution)/shard_map/ppermute | solution.py:309

commit v6 on v5

--- a/solution.py
+++ b/solution.py
@@ -22,7 +22,7 @@
 CYCLE = 8
 PARTS = 4
 STEPS = 2
-ROUNDS = ({2: 0}, {3: 0}, {0: 3, 1: 0, 3: 1}, {0: 1}, {0: 2, 1: 3, 2: 1}, {3: 2}, {1: 2, 2: 3})
+ROUNDS = ({0: 0, 2: 2, 3: 3}, {2: 0, 3: 1}, {0: 1, 1: 0}, {0: 2, 1: 3, 2: 1, 3: 0}, {0: 3, 1: 2}, {1: 1, 2: 3, 3: 2})
 BLOCK = 8
 SCREEN = 0.3
 
@@ -69,44 +69,36 @@
     return 4.0 * math.pi / (total + SCREEN * SCREEN) / float(GRID**3)
 
 
-def gather_body(s_ref, t_ref, out_ref, raw, rows, pieces, ready, arrived, left):
-    copies = []
-    for which, ref in enumerate((s_ref, t_ref)):
-        for part in range(PARTS):
-            here = pl.ds(part * GRID**3 // PARTS, GRID**3 // PARTS)
-            copies.append(pltpu.make_async_copy(ref.at[:, here], raw.at[which, :, here], arrived.at[which, part]))
-    for copy in copies:
-        copy.start()
+def gather_body(flat_ref, out_ref, raw, rows, pieces, ready, arrived, left):
+    copy = pltpu.make_async_copy(flat_ref, raw, arrived)
+    copy.start()
+    copy.wait()
     lane = lax.broadcasted_iota(jnp.int32, (PIECES // CYCLE, LANES), 1)
     period = CYCLE * PIECE // LANES
-    for which in range(2):
-        for copy in copies[which * PARTS : (which + 1) * PARTS]:
-            copy.wait()
-        rows[:FLAT, :] = raw[which].astype(jnp.float32).reshape(FLAT, LANES)
-        rows[FLAT:, :] = jnp.zeros((rows.shape[0] - FLAT, LANES), jnp.float32)
-        for piece in range(CYCLE):
-            for tile in range(TILES):
-                row, shift = divmod(PIECE * piece + LANES * tile, LANES)
-                value = rows[pl.ds(row, PIECES // CYCLE, stride=period), :]
-                if shift:
-                    after = rows[pl.ds(row + 1, PIECES // CYCLE, stride=period), :]
-                    value = pltpu.roll(jnp.where(lane >= shift, value, after), LANES - shift, 1)
-                pieces[which, tile, pl.ds(piece, PIECES // CYCLE, stride=CYCLE), :] = value
+    rows[:FLAT, :] = raw[...].astype(jnp.float32).reshape(FLAT, LANES)
+    rows[FLAT:, :] = jnp.zeros((rows.shape[0] - FLAT, LANES), jnp.float32)
+    for piece in range(CYCLE):
         for tile in range(TILES):
-            ready[which, :, tile * LANES : (tile + 1) * LANES] = pieces[which, tile].astype(jnp.bfloat16)
-        copies.append(pltpu.make_async_copy(ready.at[which], out_ref.at[pl.ds(which * PIECES, PIECES)], left.at[which]))
-        copies[-1].start()
-    for copy in copies[-2:]:
-        copy.wait()
-
-
-def body(own_ref, came_ref, kern_ref, fwd_ref, inv_ref, first_ref, last_ref, out_ref, xs, near, real, imag, real_back, imag_back, back, ys, flat, sums):
+            row, shift = divmod(PIECE * piece + LANES * tile, LANES)
+            value = rows[pl.ds(row, PIECES // CYCLE, stride=period), :]
+            if shift:
+                after = rows[pl.ds(row + 1, PIECES // CYCLE, stride=period), :]
+                value = pltpu.roll(jnp.where(lane >= shift, value, after), LANES - shift, 1)
+            pieces[tile, pl.ds(piece, PIECES // CYCLE, stride=CYCLE), :] = value
+    for tile in range(TILES):
+        ready[:, tile * LANES : (tile + 1) * LANES] = pieces[tile].astype(jnp.bfloat16)
+    copy = pltpu.make_async_copy(ready, out_ref, left)
+    copy.start()
+    copy.wait()
+
+
+def body(own_ref, came_ref, t_ref, kern_ref, fwd_ref, inv_ref, first_ref, last_ref, out_ref, xs, near, real, imag, real_back, imag_back, back, ys, flat, sums):
     lane = lax.broadcasted_iota(jnp.int32, (PIECES, LANES), 1)
     low = lane < HALF
 
-    target = came_ref[PIECES:, :]
-    flat[0] = own_ref[:PIECES, :] * target
-    flat[1] = came_ref[:PIECES, :] * target
+    target = t_ref[...]
+    flat[0] = own_ref[...] * target
+    flat[1] = came_ref[...] * target
 
     def aligned(which, group, to):
         start = GRID * group
@@ -195,8 +187,8 @@
                 tiles[which][tile + 1] = moved
     for tile in range(TILES):
         here = slice(tile * LANES, (tile + 1) * LANES)
-        total = own_ref[:PIECES, here].astype(jnp.float32) * tiles[0][tile].astype(jnp.float32)
-        total += came_ref[:PIECES, here].astype(jnp.float32) * tiles[1][tile].astype(jnp.float32)
+        total = own_ref[:, here].astype(jnp.float32) * tiles[0][tile].astype(jnp.float32)
+        total += came_ref[:, here].astype(jnp.float32) * tiles[1][tile].astype(jnp.float32)
         for part in range(PARTS):
             sums[pl.ds(part * TILES + tile, BLOCK, stride=PARTS * TILES), :] = -total[part * BLOCK : (part + 1) * BLOCK]
     out_ref[...] = sums[...].astype(jnp.bfloat16)
@@ -206,32 +198,32 @@
 PARAMS = pltpu.CompilerParams(vmem_limit_bytes=16 * 2**20)
 
 
-def gathered(sources, targets):
+def gathered(block):
     return pl.pallas_call(
         gather_body,
-        out_shape=jax.ShapeDtypeStruct((2 * PIECES, WIDE), jnp.bfloat16),
-        in_specs=[pl.BlockSpec(memory_space=pltpu.HBM)] * 2,
+        out_shape=jax.ShapeDtypeStruct((PIECES, WIDE), jnp.bfloat16),
+        in_specs=[pl.BlockSpec(memory_space=pltpu.HBM)],
         out_specs=pl.BlockSpec(memory_space=pltpu.HBM),
         scratch_shapes=[
-            pltpu.VMEM((2, 1, GRID**3), jnp.bfloat16),
+            pltpu.VMEM((1, GRID**3), jnp.bfloat16),
             pltpu.VMEM((FLAT + 4, LANES), jnp.float32),
-            pltpu.VMEM((2, TILES, PIECES, LANES), jnp.float32),
-            pltpu.VMEM((2, PIECES, WIDE), jnp.bfloat16),
-            pltpu.SemaphoreType.DMA((2, PARTS)),
-            pltpu.SemaphoreType.DMA((2,)),
+            pltpu.VMEM((TILES, PIECES, LANES), jnp.float32),
+            pltpu.VMEM((PIECES, WIDE), jnp.bfloat16),
+            pltpu.SemaphoreType.DMA,
+            pltpu.SemaphoreType.DMA,
         ],
         compiler_params=pltpu.CompilerParams(vmem_limit_bytes=61000 * 1024),
         cost_estimate=pl.CostEstimate(flops=1_000_000, bytes_accessed=800_000, transcendentals=0),
         name="gather",
-    )(sources, targets)
-
-
-def exchange_term(own, came):
+    )(block)
+
+
+def exchange_term(own, came, target):
     constants = [jnp.asarray(w, jnp.bfloat16) for w in weights()]
     return pl.pallas_call(
         body,
         out_shape=jax.ShapeDtypeStruct((PIECES * TILES, LANES), jnp.bfloat16),
-        in_specs=[VMEM] * 7,
+        in_specs=[VMEM] * 8,
         out_specs=VMEM,
         scratch_shapes=[
             *[pltpu.VMEM((ROWS, LANES), jnp.float32)] * 8,
@@ -241,22 +233,21 @@
         compiler_params=PARAMS,
         cost_estimate=pl.CostEstimate(flops=200_000_000, bytes_accessed=2_000_000, transcendentals=0),
         name="exchange",
-    )(own, came, kernel_table(), *constants)
-
-
-def from_behind(block):
+    )(own, came, target, kernel_table(), *constants)
+
+
+def from_ahead(block):
     count = lax.axis_size("blk")
-    return lax.ppermute(block, "blk", [((i - 1) % count, i) for i in range(count)])
-
-
-def block_sum_body(came_ref, own_ref, *refs):
+    return lax.ppermute(block, "blk", [((i + 1) % count, i) for i in range(count)])
+
+
+def block_sum_body(came_ref, *refs):
     *out_refs, held = refs
     total = came_ref[0].astype(jnp.float32)
     for other in range(1, BLOCK):
         total += came_ref[other].astype(jnp.float32)
     held[...] = total
     part = lax.div(lax.axis_index("wide"), BLOCK)
-    own_ref[...] = held[pl.ds(pl.multiple_of(part * TILES, TILES), TILES), :]
     for ends, out_ref in zip(ROUNDS, out_refs, strict=True):
         end = jnp.int32(0)
         for start, chosen in ends.items():
@@ -268,9 +259,9 @@
     shape = (TILES, LANES)
     return pl.pallas_call(
         block_sum_body,
-        out_shape=[jax.ShapeDtypeStruct(shape, jnp.float32)] + [jax.ShapeDtypeStruct(shape, jnp.bfloat16)] * len(ROUNDS),
+        out_shape=[jax.ShapeDtypeStruct(shape, jnp.bfloat16)] * len(ROUNDS),
         in_specs=[VMEM],
-        out_specs=[VMEM] * (1 + len(ROUNDS)),
+        out_specs=[VMEM] * len(ROUNDS),
         scratch_shapes=[pltpu.VMEM((PARTS * TILES, LANES), jnp.float32)],
         compiler_params=PARAMS,
         cost_estimate=pl.CostEstimate(flops=100_000, bytes_accessed=150_000, transcendentals=0),
@@ -278,36 +269,38 @@
     )(came)
 
 
-def last_sum_body(own_ref, *refs):
-    total = own_ref[...]
-    for ref in refs[:-1]:
+def last_sum_body(*refs):
+    total = refs[0][...].astype(jnp.float32)
+    for ref in refs[1:-1]:
         total += ref[...].astype(jnp.float32)
     refs[-1][...] = total
 
 
-def last_sum(own, came):
+def last_sum(came):
     return pl.pallas_call(
         last_sum_body,
         out_shape=jax.ShapeDtypeStruct((TILES, LANES), jnp.float32),
-        in_specs=[VMEM] * (1 + len(came)),
+        in_specs=[VMEM] * len(came),
         out_specs=VMEM,
         compiler_params=PARAMS,
         cost_estimate=pl.CostEstimate(flops=100_000, bytes_accessed=80_000, transcendentals=0),
         name="last_sum",
-    )(own, *came)
+    )(*came)
 
 
 def shards(sources, targets):
-    own = gathered(sources, targets)
-    partial = exchange_term(own, from_behind(own))
+    blk = lax.axis_size("blk")
+    own = gathered(sources)
+    partial = exchange_term(own, from_ahead(own), gathered(targets))
     groups = [[part * BLOCK + i for i in range(BLOCK)] for part in range(PARTS)]
     came = lax.all_to_all(partial, "wide", split_axis=0, concat_axis=0, axis_index_groups=groups, tiled=True)
-    mine, *sent = block_sum(came.reshape(BLOCK, PARTS * TILES, LANES))
+    sent = block_sum(came.reshape(BLOCK, PARTS * TILES, LANES))
     arrived = []
     for turn, ends in enumerate(ROUNDS):
-        route = [(start * BLOCK + i, end * BLOCK + i) for start, end in ends.items() for i in range(BLOCK)]
-        arrived.append(lax.ppermute(sent[turn], "wide", route))
-    return last_sum(mine, arrived).reshape(1, -1)[:, :PIECE]
+        pairs = [(start * BLOCK + i, end * BLOCK + i) for start, end in ends.items() for i in range(BLOCK)]
+        route = [(near * blk + b, far * blk + (b + 1) % blk) for near, far in pairs for b in range(blk)]
+        arrived.append(lax.ppermute(sent[turn], ("wide", "blk"), route))
+    return last_sum(arrived).reshape(1, -1)[:, :PIECE]
 
 
 def solution(mesh):

time: 51.8 us -> 51.6 us (level)
  the two profiles are of different devices: /device:TPU:384 before, /device:TPU:96 now
where the time goes in v6:
time: 51.6 us; the launch traced here: 51.2 us
  starting transfers between devices  32.4 us (63%)
  blocking collectives  10.2 us (20%)
  Pallas kernels  6.66 us (13%)
  waiting for transfers between devices  1.34 us (3%)
    ppermute x6, starting transfers between devices, shards(): arrived.append(lax.ppermute(sent[turn], ('wide', 'blk'), route))  27.9 us
    all_to_all x1, blocking collectives, shards(): lax.all_to_all(partial, 'wide', split_axis=0, concat_axis=0, axis_index_g...  10.2 us
    ppermute x1, starting transfers between devices, from_ahead(): lax.ppermute(block, 'blk', [((i + 1) % count, i) for i in range(count)])  4.47 us
    pallas_call x2, Pallas kernels, gathered(): pl.pallas_call(gather_body, out_shape=jax.ShapeDtypeStruct((PIECES, WIDE)...  3.67 us
    pallas_call x1, Pallas kernels, exchange_term(): pl.pallas_call(body, out_shape=jax.ShapeDtypeStruct((PIECES * TILES, LANE...  2.35 us
  transfers between devices with their start and end apart: 7, of which 2 were waited for; matrix products, arithmetic and copies ran while one was open for 1% of the time, Pallas kernels for 4%

profile of v6, /device:TPU:96, one launch (start us, length us, event | category | flops | bytes accessed | tf_op | source)
XLA Modules:
  0.0 51.2 jit_solution(13794974845513176116)
XLA Ops:
  0.0 1.8 %gather.2.own_ref = bf16[32,2048]{1,0:T(8,128)(2,1)} custom-call(bf16[1,64000]{1,0:T(2,128)(2,1)} %flat_ref.2), custom_call_target="tpu_custom_call" | custom-call | flops 1000000 | bytes 800000 | tf_op jit(solution)/shard_map/gather/pallas_call | solution.py:202
  1.8 4.5 %collective-permute-start = (bf16[32,2048]{1,0:T(8,128)(2,1)}, bf16[32,2048]{1,0:T(8,128)(2,1)S(1)}, u32[]{:S(2)}, u32[]{:S(2)}) collective-permute-start(bf16[32,2048]{1,0:T(8,128)(2,1)} %gather.2.own_ref), channel_id=1, source_target_pairs={{1,0},{2,1},{3,2},{4,3},{5,4},{6,5},{7,6},{8,7},{9,8},{10,9},{11,1... | collective-permute-start | bytes 393224 | tf_op jit(solution)/shard_map/ppermute | solution.py:241
  6.4 0.1 broadcast_add_fusion
  6.4 1.8 %gather.3.t_ref = bf16[32,2048]{1,0:T(8,128)(2,1)} custom-call(bf16[1,64000]{1,0:T(2,128)(2,1)} %flat_ref.3), custom_call_target="tpu_custom_call" | custom-call | flops 1000000 | bytes 800000 | tf_op jit(solution)/shard_map/gather/pallas_call | solution.py:202
  8.3 0.0 copy-start
  8.3 0.0 copy-start.1
  8.3 0.0 copy-start.2
  8.3 0.0 copy-start.3
  8.3 0.0 copy-start.4
  8.3 0.0 copy-start.5
  8.3 0.3 divide_multiply_fusion.kern_ref
  8.6 0.7 %collective-permute-done.came_ref = bf16[32,2048]{1,0:T(8,128)(2,1)S(1)} collective-permute-done((bf16[32,2048]{1,0:T(8,128)(2,1)}, bf16[32,2048]{1,0:T(8,128)(2,1)S(1)}, u32[]{:S(2)}, u32[]{:S(2)}) %collective-permute-start) | collective-permute-done | bytes 131104 | tf_op jit(solution)/shard_map/ppermute | solution.py:241
  9.4 0.0 copy-done
  9.4 0.0 copy-done.1
  9.4 0.0 copy-done.2
  9.4 0.0 copy-done.3
  9.4 0.0 copy-done.4
  9.4 2.4 %exchange.1 = bf16[512,128]{1,0:T(8,128)(2,1)S(1)} custom-call(bf16[32,2048]{1,0:T(8,128)(2,1)S(1)} %copy-done, bf16[32,2048]{1,0:T(8,128)(2,1)S(1)} %collective-permute-done.came_ref, bf16[32,2048]{1,0:T(8,128)(2,1)S(1)} %copy-done.1, f32[40,40,128]{2,1,0:T(8,128)S(1)} %divide_multiply_fusion.kern_ref, bf16[80,80]{1,0:T(8,128)(2,1)S(1)} %copy-done.5, ...), custom_call_target="tpu_custom_call" | custom-call | flops 200000000 | bytes 2000000 | tf_op jit(solution)/shard_map/exchange/pallas_call | solution.py:223
  11.8 10.2 %all_to_all.9.came_ref = bf16[8,64,128]{2,1,0:T(8,128)(2,1)S(1)} all-to-all(bf16[8,64,128]{2,1,0:T(8,128)(2,1)S(1)} %bitcast.3), channel_id=1, replica_groups={{0,16,32,48,64,80,96,112},{128,144,160,176,192,208,224,240},{256,272,28..., dimensions={0} | all-to-all | bytes 262144 | tf_op jit(solution)/shard_map/all_to_all | solution.py:296
  22.0 3.3 %collective-permute-start.1 = (bf16[16,128]{1,0:T(8,128)(2,1)S(1)}, bf16[16,128]{1,0:T(8,128)(2,1)S(1)}, u32[]{:S(2)}, u32[]{:S(2)}) collective-permute-start(bf16[16,128]{1,0:T(8,128)(2,1)S(1)} %get-tuple-element.11), channel_id=1, source_target_pairs={{0,1},{1,2},{2,3},{3,4},{4,5},{5,6},{6,7},{7,8},{8,9},{9,10},{10,1... | collective-permute-start | bytes 12296 | tf_op jit(solution)/shard_map/ppermute | solution.py:302
  25.3 1.3 %collective-permute-start.2 = (bf16[16,128]{1,0:T(8,128)(2,1)S(1)}, bf16[16,128]{1,0:T(8,128)(2,1)S(1)}, u32[]{:S(2)}, u32[]{:S(2)}) collective-permute-start(bf16[16,128]{1,0:T(8,128)(2,1)S(1)} %get-tuple-element.12), channel_id=1, source_target_pairs={{256,1},{257,2},{258,3},{259,4},{260,5},{261,6},{262,7},{263,8},{2... | collective-permute-start | bytes 12296 | tf_op jit(solution)/shard_map/ppermute | solution.py:302
  26.6 7.3 %collective-permute-start.3 = (bf16[16,128]{1,0:T(8,128)(2,1)S(1)}, bf16[16,128]{1,0:T(8,128)(2,1)S(1)}, u32[]{:S(2)}, u32[]{:S(2)}) collective-permute-start(bf16[16,128]{1,0:T(8,128)(2,1)S(1)} %get-tuple-element.13), channel_id=1, source_target_pairs={{0,129},{1,130},{2,131},{3,132},{4,133},{5,134},{6,135},{7,136},{8... | collective-permute-start | bytes 12296 | tf_op jit(solution)/shard_map/ppermute | solution.py:302
  33.9 12.3 %collective-permute-start.4 = (bf16[16,128]{1,0:T(8,128)(2,1)S(1)}, bf16[16,128]{1,0:T(8,128)(2,1)S(1)}, u32[]{:S(2)}, u32[]{:S(2)}) collective-permute-start(bf16[16,128]{1,0:T(8,128)(2,1)S(1)} %get-tuple-element.14), channel_id=1, source_target_pairs={{0,257},{1,258},{2,259},{3,260},{4,261},{5,262},{6,263},{7,264},{8... | collective-permute-start | bytes 12296 | tf_op jit(solution)/shard_map/ppermute | solution.py:302
  46.2 3.1 %collective-permute-start.5 = (bf16[16,128]{1,0:T(8,128)(2,1)S(1)}, bf16[16,128]{1,0:T(8,128)(2,1)S(1)}, u32[]{:S(2)}, u32[]{:S(2)}) collective-permute-start(bf16[16,128]{1,0:T(8,128)(2,1)S(1)} %get-tuple-element.15), channel_id=1, source_target_pairs={{0,385},{1,386},{2,387},{3,388},{4,389},{5,390},{6,391},{7,392},{8... | collective-permute-start | bytes 12296 | tf_op jit(solution)/shard_map/ppermute | solution.py:302
  49.3 0.0 collective-permute-done.1.refs_0_
  49.3 0.7 %collective-permute-start.6 = (bf16[16,128]{1,0:T(8,128)(2,1)S(1)}, bf16[16,128]{1,0:T(8,128)(2,1)S(1)}, u32[]{:S(2)}, u32[]{:S(2)}) collective-permute-start(bf16[16,128]{1,0:T(8,128)(2,1)S(1)} %get-tuple-element.16), channel_id=1, source_target_pairs={{128,129},{129,130},{130,131},{131,132},{132,133},{133,134},{134,1... | collective-permute-start | bytes 12296 | tf_op jit(solution)/shard_map/ppermute | solution.py:302
  50.0 0.0 collective-permute-done.2.refs_1_
  50.0 0.0 collective-permute-done.3.refs_2_
  50.0 0.0 collective-permute-done.4.refs_3_
  50.0 0.6 %collective-permute-done.5.refs_4_ = bf16[16,128]{1,0:T(8,128)(2,1)S(1)} collective-permute-done((bf16[16,128]{1,0:T(8,128)(2,1)S(1)}, bf16[16,128]{1,0:T(8,128)(2,1)S(1)}, u32[]{:S(2)}, u32[]{:S(2)}) %collective-permute-start.5) | collective-permute-done | bytes 4128 | tf_op jit(solution)/shard_map/ppermute | solution.py:302
  50.6 0.0 collective-permute-done.6.refs_5_
  50.6 0.6 %last_sum.1 = f32[16,128]{1,0:T(8,128)} custom-call(bf16[16,128]{1,0:T(8,128)(2,1)S(1)} %collective-permute-done.1.refs_0_, bf16[16,128]{1,0:T(8,128)(2,1)S(1)} %collective-permute-done.2.refs_1_, bf16[16,128]{1,0:T(8,128)(2,1)S(1)} %collective-permute-done.3.refs_2_, bf16[16,128]{1,0:T(8,128)(2,1)S(1)} %collective-permute-done.4.refs_3_, ...), custom_call_target="tpu_custom_call" | custom-call | flops 100000 | bytes 80000 | tf_op jit(solution)/shard_map/last_sum/pallas_call | solution.py:280
  (4 shorter events, 0.1 us)
Async XLA Ops:
  1.8 7.5 %collective-permute-start = (bf16[32,2048]{1,0:T(8,128)(2,1)}, bf16[32,2048]{1,0:T(8,128)(2,1)S(1)}, u32[]{:S(2)}, u32[]{:S(2)}) collective-permute-start(bf16[32,2048]{1,0:T(8,128)(2,1)} %gather.2.own_ref), channel_id=1, source_target_pairs={{1,0},{2,1},{3,2},{4,3},{5,4},{6,5},{7,6},{8,7},{9,8},{10,9},{11,1... | collective-permute-start | bytes 393224 | tf_op jit(solution)/shard_map/ppermute | solution.py:241
  8.3 1.1 %copy-start = (bf16[32,2048]{1,0:T(8,128)(2,1)S(1)}, bf16[32,2048]{1,0:T(8,128)(2,1)}, u32[]{:S(2)}) copy-start(bf16[32,2048]{1,0:T(8,128)(2,1)} %gather.2.own_ref) | copy-start | bytes 393220
  8.3 1.1 %copy-start.1 = (bf16[32,2048]{1,0:T(8,128)(2,1)S(1)}, bf16[32,2048]{1,0:T(8,128)(2,1)}, u32[]{:S(2)}) copy-start(bf16[32,2048]{1,0:T(8,128)(2,1)} %gather.3.t_ref) | copy-start | bytes 393220
  8.3 1.1 %copy-start.2 = (bf16[256,256]{1,0:T(8,128)(2,1)S(1)}, bf16[256,256]{1,0:T(8,128)(2,1)}, u32[]{:S(2)}) copy-start(bf16[256,256]{1,0:T(8,128)(2,1)} %constant.48.clone.last_ref) | copy-start | bytes 393220
  8.3 1.1 %copy-start.3 = (bf16[256,256]{1,0:T(8,128)(2,1)S(1)}, bf16[256,256]{1,0:T(8,128)(2,1)}, u32[]{:S(2)}) copy-start(bf16[256,256]{1,0:T(8,128)(2,1)} %constant.47.clone.first_ref) | copy-start | bytes 393220
  8.3 1.1 %copy-start.4 = (bf16[80,80]{1,0:T(8,128)(2,1)S(1)}, bf16[80,80]{1,0:T(8,128)(2,1)}, u32[]{:S(2)}) copy-start(bf16[80,80]{1,0:T(8,128)(2,1)} %constant.46.clone.inv_ref) | copy-start | bytes 38404
  8.3 1.1 %copy-start.5 = (bf16[80,80]{1,0:T(8,128)(2,1)S(1)}, bf16[80,80]{1,0:T(8,128)(2,1)}, u32[]{:S(2)}) copy-start(bf16[80,80]{1,0:T(8,128)(2,1)} %constant.45.clone.fwd_ref) | copy-start | bytes 38404
  22.0 27.3 %collective-permute-start.1 = (bf16[16,128]{1,0:T(8,128)(2,1)S(1)}, bf16[16,128]{1,0:T(8,128)(2,1)S(1)}, u32[]{:S(2)}, u32[]{:S(2)}) collective-permute-start(bf16[16,128]{1,0:T(8,128)(2,1)S(1)} %get-tuple-element.11), channel_id=1, source_target_pairs={{0,1},{1,2},{2,3},{3,4},{4,5},{5,6},{6,7},{7,8},{8,9},{9,10},{10,1... | collective-permute-start | bytes 12296 | tf_op jit(solution)/shard_map/ppermute | solution.py:302
  25.3 24.7 %collective-permute-start.2 = (bf16[16,128]{1,0:T(8,128)(2,1)S(1)}, bf16[16,128]{1,0:T(8,128)(2,1)S(1)}, u32[]{:S(2)}, u32[]{:S(2)}) collective-permute-start(bf16[16,128]{1,0:T(8,128)(2,1)S(1)} %get-tuple-element.12), channel_id=1, source_target_pairs={{256,1},{257,2},{258,3},{259,4},{260,5},{261,6},{262,7},{263,8},{2... | collective-permute-start | bytes 12296 | tf_op jit(solution)/shard_map/ppermute | solution.py:302
  26.6 23.4 %collective-permute-start.3 = (bf16[16,128]{1,0:T(8,128)(2,1)S(1)}, bf16[16,128]{1,0:T(8,128)(2,1)S(1)}, u32[]{:S(2)}, u32[]{:S(2)}) collective-permute-start(bf16[16,128]{1,0:T(8,128)(2,1)S(1)} %get-tuple-element.13), channel_id=1, source_target_pairs={{0,129},{1,130},{2,131},{3,132},{4,133},{5,134},{6,135},{7,136},{8... | collective-permute-start | bytes 12296 | tf_op jit(solution)/shard_map/ppermute | solution.py:302
  33.9 16.1 %collective-permute-start.4 = (bf16[16,128]{1,0:T(8,128)(2,1)S(1)}, bf16[16,128]{1,0:T(8,128)(2,1)S(1)}, u32[]{:S(2)}, u32[]{:S(2)}) collective-permute-start(bf16[16,128]{1,0:T(8,128)(2,1)S(1)} %get-tuple-element.14), channel_id=1, source_target_pairs={{0,257},{1,258},{2,259},{3,260},{4,261},{5,262},{6,263},{7,264},{8... | collective-permute-start | bytes 12296 | tf_op jit(solution)/shard_map/ppermute | solution.py:302
  46.2 4.4 %collective-permute-start.5 = (bf16[16,128]{1,0:T(8,128)(2,1)S(1)}, bf16[16,128]{1,0:T(8,128)(2,1)S(1)}, u32[]{:S(2)}, u32[]{:S(2)}) collective-permute-start(bf16[16,128]{1,0:T(8,128)(2,1)S(1)} %get-tuple-element.15), channel_id=1, source_target_pairs={{0,385},{1,386},{2,387},{3,388},{4,389},{5,390},{6,391},{7,392},{8... | collective-permute-start | bytes 12296 | tf_op jit(solution)/shard_map/ppermute | solution.py:302
  49.3 1.3 %collective-permute-start.6 = (bf16[16,128]{1,0:T(8,128)(2,1)S(1)}, bf16[16,128]{1,0:T(8,128)(2,1)S(1)}, u32[]{:S(2)}, u32[]{:S(2)}) collective-permute-start(bf16[16,128]{1,0:T(8,128)(2,1)S(1)} %get-tuple-element.16), channel_id=1, source_target_pairs={{128,129},{129,130},{130,131},{131,132},{132,133},{133,134},{134,1... | collective-permute-start | bytes 12296 | tf_op jit(solution)/shard_map/ppermute | solution.py:302

commit v7 on v6

--- a/solution.py
+++ b/solution.py
@@ -94,24 +94,28 @@
 
 def body(own_ref, came_ref, t_ref, kern_ref, fwd_ref, inv_ref, first_ref, last_ref, out_ref, xs, near, real, imag, real_back, imag_back, back, ys, flat, sums):
     lane = lax.broadcasted_iota(jnp.int32, (PIECES, LANES), 1)
-    low = lane < HALF
 
     target = t_ref[...]
     flat[0] = own_ref[...] * target
     flat[1] = came_ref[...] * target
 
-    def aligned(which, group, to):
-        start = GRID * group
-        tile, shift = start // LANES, start % LANES
+    turned_lane = lax.rem(lane + HALF, LANES)
+    for tile in range(TILES):
+        here = slice(tile * LANES, (tile + 1) * LANES)
+        flat[1, :, here] = pltpu.roll(flat[1, :, here], HALF, 1)
+
+    def window(which, tile, shift, place):
         value = flat[which, :, tile * LANES : (tile + 1) * LANES]
         if shift + GRID > LANES:
-            after = flat[which, :, (tile + 1) * LANES : (tile + 2) * LANES]
-            value = jnp.where(lane >= shift, value, after)
-        turn = (to - shift) % LANES
-        return pltpu.roll(value, turn, 1) if turn else value
+            value = jnp.where(place >= shift, value, flat[which, :, (tile + 1) * LANES : (tile + 2) * LANES])
+        return value
 
     for group in range(GROUPS):
-        merged = jnp.where(low, aligned(0, group, 0), aligned(1, group, HALF))
+        tile, shift = divmod(GRID * group, LANES)
+        first_half = lax.rem(lane + (LANES - shift), LANES) < HALF
+        merged = jnp.where(first_half, window(0, tile, shift, lane), window(1, tile, shift, turned_lane))
+        if shift:
+            merged = pltpu.roll(merged, LANES - shift, 1)
         xs[pl.ds(group, PIECES, stride=GROUPS), :] = merged.astype(jnp.float32)
 
     forward, inverse = fwd_ref[...], inv_ref[...]

time: 51.6 us -> 51.5 us (level)
  no operation moved by 1% of the time
where the time goes in v7:
time: 51.5 us; the launch traced here: 51.2 us
  starting transfers between devices  32.4 us (63%)
  blocking collectives  10.2 us (20%)
  Pallas kernels  6.65 us (13%)
  waiting for transfers between devices  1.34 us (3%)
    ppermute x6, starting transfers between devices, shards(): arrived.append(lax.ppermute(sent[turn], ('wide', 'blk'), route))  27.9 us
    all_to_all x1, blocking collectives, shards(): lax.all_to_all(partial, 'wide', split_axis=0, concat_axis=0, axis_index_g...  10.2 us
    ppermute x1, starting transfers between devices, from_ahead(): lax.ppermute(block, 'blk', [((i + 1) % count, i) for i in range(count)])  4.47 us
    pallas_call x2, Pallas kernels, gathered(): pl.pallas_call(gather_body, out_shape=jax.ShapeDtypeStruct((PIECES, WIDE)...  3.67 us
    pallas_call x1, Pallas kernels, exchange_term(): pl.pallas_call(body, out_shape=jax.ShapeDtypeStruct((PIECES * TILES, LANE...  2.34 us
  transfers between devices with their start and end apart: 7, of which 2 were waited for; matrix products, arithmetic and copies ran while one was open for 1% of the time, Pallas kernels for 4%

profile of v7, /device:TPU:96, one launch (start us, length us, event | category | flops | bytes accessed | tf_op | source)
XLA Modules:
  0.0 51.2 jit_solution(7793035267693980503)
XLA Ops:
  0.0 1.8 %gather.2.own_ref = bf16[32,2048]{1,0:T(8,128)(2,1)} custom-call(bf16[1,64000]{1,0:T(2,128)(2,1)} %flat_ref.2), custom_call_target="tpu_custom_call" | custom-call | flops 1000000 | bytes 800000 | tf_op jit(solution)/shard_map/gather/pallas_call | solution.py:206
  1.8 4.5 %collective-permute-start = (bf16[32,2048]{1,0:T(8,128)(2,1)}, bf16[32,2048]{1,0:T(8,128)(2,1)S(1)}, u32[]{:S(2)}, u32[]{:S(2)}) collective-permute-start(bf16[32,2048]{1,0:T(8,128)(2,1)} %gather.2.own_ref), channel_id=1, source_target_pairs={{1,0},{2,1},{3,2},{4,3},{5,4},{6,5},{7,6},{8,7},{9,8},{10,9},{11,1... | collective-permute-start | bytes 393224 | tf_op jit(solution)/shard_map/ppermute | solution.py:245
  6.4 0.1 broadcast_add_fusion
  6.4 1.8 %gather.3.t_ref = bf16[32,2048]{1,0:T(8,128)(2,1)} custom-call(bf16[1,64000]{1,0:T(2,128)(2,1)} %flat_ref.3), custom_call_target="tpu_custom_call" | custom-call | flops 1000000 | bytes 800000 | tf_op jit(solution)/shard_map/gather/pallas_call | solution.py:206
  8.3 0.0 copy-start
  8.3 0.0 copy-start.1
  8.3 0.0 copy-start.2
  8.3 0.0 copy-start.3
  8.3 0.0 copy-start.4
  8.3 0.0 copy-start.5
  8.3 0.3 divide_multiply_fusion.kern_ref
  8.6 0.7 %collective-permute-done.came_ref = bf16[32,2048]{1,0:T(8,128)(2,1)S(1)} collective-permute-done((bf16[32,2048]{1,0:T(8,128)(2,1)}, bf16[32,2048]{1,0:T(8,128)(2,1)S(1)}, u32[]{:S(2)}, u32[]{:S(2)}) %collective-permute-start) | collective-permute-done | bytes 131104 | tf_op jit(solution)/shard_map/ppermute | solution.py:245
  9.4 0.0 copy-done
  9.4 0.0 copy-done.1
  9.4 0.0 copy-done.2
  9.4 0.0 copy-done.3
  9.4 0.0 copy-done.4
  9.4 2.3 %exchange.1 = bf16[512,128]{1,0:T(8,128)(2,1)S(1)} custom-call(bf16[32,2048]{1,0:T(8,128)(2,1)S(1)} %copy-done, bf16[32,2048]{1,0:T(8,128)(2,1)S(1)} %collective-permute-done.came_ref, bf16[32,2048]{1,0:T(8,128)(2,1)S(1)} %copy-done.1, f32[40,40,128]{2,1,0:T(8,128)S(1)} %divide_multiply_fusion.kern_ref, bf16[80,80]{1,0:T(8,128)(2,1)S(1)} %copy-done.5, ...), custom_call_target="tpu_custom_call" | custom-call | flops 200000000 | bytes 2000000 | tf_op jit(solution)/shard_map/exchange/pallas_call | solution.py:227
  11.8 10.2 %all_to_all.9.came_ref = bf16[8,64,128]{2,1,0:T(8,128)(2,1)S(1)} all-to-all(bf16[8,64,128]{2,1,0:T(8,128)(2,1)S(1)} %bitcast.3), channel_id=1, replica_groups={{0,16,32,48,64,80,96,112},{128,144,160,176,192,208,224,240},{256,272,28..., dimensions={0} | all-to-all | bytes 262144 | tf_op jit(solution)/shard_map/all_to_all | solution.py:300
  22.0 3.3 %collective-permute-start.1 = (bf16[16,128]{1,0:T(8,128)(2,1)S(1)}, bf16[16,128]{1,0:T(8,128)(2,1)S(1)}, u32[]{:S(2)}, u32[]{:S(2)}) collective-permute-start(bf16[16,128]{1,0:T(8,128)(2,1)S(1)} %get-tuple-element.11), channel_id=1, source_target_pairs={{0,1},{1,2},{2,3},{3,4},{4,5},{5,6},{6,7},{7,8},{8,9},{9,10},{10,1... | collective-permute-start | bytes 12296 | tf_op jit(solution)/shard_map/ppermute | solution.py:306
  25.3 1.3 %collective-permute-start.2 = (bf16[16,128]{1,0:T(8,128)(2,1)S(1)}, bf16[16,128]{1,0:T(8,128)(2,1)S(1)}, u32[]{:S(2)}, u32[]{:S(2)}) collective-permute-start(bf16[16,128]{1,0:T(8,128)(2,1)S(1)} %get-tuple-element.12), channel_id=1, source_target_pairs={{256,1},{257,2},{258,3},{259,4},{260,5},{261,6},{262,7},{263,8},{2... | collective-permute-start | bytes 12296 | tf_op jit(solution)/shard_map/ppermute | solution.py:306
  26.6 7.3 %collective-permute-start.3 = (bf16[16,128]{1,0:T(8,128)(2,1)S(1)}, bf16[16,128]{1,0:T(8,128)(2,1)S(1)}, u32[]{:S(2)}, u32[]{:S(2)}) collective-permute-start(bf16[16,128]{1,0:T(8,128)(2,1)S(1)} %get-tuple-element.13), channel_id=1, source_target_pairs={{0,129},{1,130},{2,131},{3,132},{4,133},{5,134},{6,135},{7,136},{8... | collective-permute-start | bytes 12296 | tf_op jit(solution)/shard_map/ppermute | solution.py:306
  33.9 12.3 %collective-permute-start.4 = (bf16[16,128]{1,0:T(8,128)(2,1)S(1)}, bf16[16,128]{1,0:T(8,128)(2,1)S(1)}, u32[]{:S(2)}, u32[]{:S(2)}) collective-permute-start(bf16[16,128]{1,0:T(8,128)(2,1)S(1)} %get-tuple-element.14), channel_id=1, source_target_pairs={{0,257},{1,258},{2,259},{3,260},{4,261},{5,262},{6,263},{7,264},{8... | collective-permute-start | bytes 12296 | tf_op jit(solution)/shard_map/ppermute | solution.py:306
  46.2 3.1 %collective-permute-start.5 = (bf16[16,128]{1,0:T(8,128)(2,1)S(1)}, bf16[16,128]{1,0:T(8,128)(2,1)S(1)}, u32[]{:S(2)}, u32[]{:S(2)}) collective-permute-start(bf16[16,128]{1,0:T(8,128)(2,1)S(1)} %get-tuple-element.15), channel_id=1, source_target_pairs={{0,385},{1,386},{2,387},{3,388},{4,389},{5,390},{6,391},{7,392},{8... | collective-permute-start | bytes 12296 | tf_op jit(solution)/shard_map/ppermute | solution.py:306
  49.3 0.0 collective-permute-done.1.refs_0_
  49.3 0.7 %collective-permute-start.6 = (bf16[16,128]{1,0:T(8,128)(2,1)S(1)}, bf16[16,128]{1,0:T(8,128)(2,1)S(1)}, u32[]{:S(2)}, u32[]{:S(2)}) collective-permute-start(bf16[16,128]{1,0:T(8,128)(2,1)S(1)} %get-tuple-element.16), channel_id=1, source_target_pairs={{128,129},{129,130},{130,131},{131,132},{132,133},{133,134},{134,1... | collective-permute-start | bytes 12296 | tf_op jit(solution)/shard_map/ppermute | solution.py:306
  50.0 0.0 collective-permute-done.2.refs_1_
  50.0 0.0 collective-permute-done.3.refs_2_
  50.0 0.0 collective-permute-done.4.refs_3_
  50.0 0.6 %collective-permute-done.5.refs_4_ = bf16[16,128]{1,0:T(8,128)(2,1)S(1)} collective-permute-done((bf16[16,128]{1,0:T(8,128)(2,1)S(1)}, bf16[16,128]{1,0:T(8,128)(2,1)S(1)}, u32[]{:S(2)}, u32[]{:S(2)}) %collective-permute-start.5) | collective-permute-done | bytes 4128 | tf_op jit(solution)/shard_map/ppermute | solution.py:306
  50.6 0.0 collective-permute-done.6.refs_5_
  50.6 0.6 %last_sum.1 = f32[16,128]{1,0:T(8,128)} custom-call(bf16[16,128]{1,0:T(8,128)(2,1)S(1)} %collective-permute-done.1.refs_0_, bf16[16,128]{1,0:T(8,128)(2,1)S(1)} %collective-permute-done.2.refs_1_, bf16[16,128]{1,0:T(8,128)(2,1)S(1)} %collective-permute-done.3.refs_2_, bf16[16,128]{1,0:T(8,128)(2,1)S(1)} %collective-permute-done.4.refs_3_, ...), custom_call_target="tpu_custom_call" | custom-call | flops 100000 | bytes 80000 | tf_op jit(solution)/shard_map/last_sum/pallas_call | solution.py:284
  (4 shorter events, 0.1 us)
Async XLA Ops:
  1.8 7.5 %collective-permute-start = (bf16[32,2048]{1,0:T(8,128)(2,1)}, bf16[32,2048]{1,0:T(8,128)(2,1)S(1)}, u32[]{:S(2)}, u32[]{:S(2)}) collective-permute-start(bf16[32,2048]{1,0:T(8,128)(2,1)} %gather.2.own_ref), channel_id=1, source_target_pairs={{1,0},{2,1},{3,2},{4,3},{5,4},{6,5},{7,6},{8,7},{9,8},{10,9},{11,1... | collective-permute-start | bytes 393224 | tf_op jit(solution)/shard_map/ppermute | solution.py:245
  8.3 1.1 %copy-start = (bf16[32,2048]{1,0:T(8,128)(2,1)S(1)}, bf16[32,2048]{1,0:T(8,128)(2,1)}, u32[]{:S(2)}) copy-start(bf16[32,2048]{1,0:T(8,128)(2,1)} %gather.2.own_ref) | copy-start | bytes 393220
  8.3 1.1 %copy-start.1 = (bf16[32,2048]{1,0:T(8,128)(2,1)S(1)}, bf16[32,2048]{1,0:T(8,128)(2,1)}, u32[]{:S(2)}) copy-start(bf16[32,2048]{1,0:T(8,128)(2,1)} %gather.3.t_ref) | copy-start | bytes 393220
  8.3 1.1 %copy-start.2 = (bf16[256,256]{1,0:T(8,128)(2,1)S(1)}, bf16[256,256]{1,0:T(8,128)(2,1)}, u32[]{:S(2)}) copy-start(bf16[256,256]{1,0:T(8,128)(2,1)} %constant.48.clone.last_ref) | copy-start | bytes 393220
  8.3 1.1 %copy-start.3 = (bf16[256,256]{1,0:T(8,128)(2,1)S(1)}, bf16[256,256]{1,0:T(8,128)(2,1)}, u32[]{:S(2)}) copy-start(bf16[256,256]{1,0:T(8,128)(2,1)} %constant.47.clone.first_ref) | copy-start | bytes 393220
  8.3 1.1 %copy-start.4 = (bf16[80,80]{1,0:T(8,128)(2,1)S(1)}, bf16[80,80]{1,0:T(8,128)(2,1)}, u32[]{:S(2)}) copy-start(bf16[80,80]{1,0:T(8,128)(2,1)} %constant.46.clone.inv_ref) | copy-start | bytes 38404
  8.3 1.1 %copy-start.5 = (bf16[80,80]{1,0:T(8,128)(2,1)S(1)}, bf16[80,80]{1,0:T(8,128)(2,1)}, u32[]{:S(2)}) copy-start(bf16[80,80]{1,0:T(8,128)(2,1)} %constant.45.clone.fwd_ref) | copy-start | bytes 38404
  22.0 27.3 %collective-permute-start.1 = (bf16[16,128]{1,0:T(8,128)(2,1)S(1)}, bf16[16,128]{1,0:T(8,128)(2,1)S(1)}, u32[]{:S(2)}, u32[]{:S(2)}) collective-permute-start(bf16[16,128]{1,0:T(8,128)(2,1)S(1)} %get-tuple-element.11), channel_id=1, source_target_pairs={{0,1},{1,2},{2,3},{3,4},{4,5},{5,6},{6,7},{7,8},{8,9},{9,10},{10,1... | collective-permute-start | bytes 12296 | tf_op jit(solution)/shard_map/ppermute | solution.py:306
  25.3 24.7 %collective-permute-start.2 = (bf16[16,128]{1,0:T(8,128)(2,1)S(1)}, bf16[16,128]{1,0:T(8,128)(2,1)S(1)}, u32[]{:S(2)}, u32[]{:S(2)}) collective-permute-start(bf16[16,128]{1,0:T(8,128)(2,1)S(1)} %get-tuple-element.12), channel_id=1, source_target_pairs={{256,1},{257,2},{258,3},{259,4},{260,5},{261,6},{262,7},{263,8},{2... | collective-permute-start | bytes 12296 | tf_op jit(solution)/shard_map/ppermute | solution.py:306
  26.6 23.4 %collective-permute-start.3 = (bf16[16,128]{1,0:T(8,128)(2,1)S(1)}, bf16[16,128]{1,0:T(8,128)(2,1)S(1)}, u32[]{:S(2)}, u32[]{:S(2)}) collective-permute-start(bf16[16,128]{1,0:T(8,128)(2,1)S(1)} %get-tuple-element.13), channel_id=1, source_target_pairs={{0,129},{1,130},{2,131},{3,132},{4,133},{5,134},{6,135},{7,136},{8... | collective-permute-start | bytes 12296 | tf_op jit(solution)/shard_map/ppermute | solution.py:306
  33.9 16.1 %collective-permute-start.4 = (bf16[16,128]{1,0:T(8,128)(2,1)S(1)}, bf16[16,128]{1,0:T(8,128)(2,1)S(1)}, u32[]{:S(2)}, u32[]{:S(2)}) collective-permute-start(bf16[16,128]{1,0:T(8,128)(2,1)S(1)} %get-tuple-element.14), channel_id=1, source_target_pairs={{0,257},{1,258},{2,259},{3,260},{4,261},{5,262},{6,263},{7,264},{8... | collective-permute-start | bytes 12296 | tf_op jit(solution)/shard_map/ppermute | solution.py:306
  46.2 4.4 %collective-permute-start.5 = (bf16[16,128]{1,0:T(8,128)(2,1)S(1)}, bf16[16,128]{1,0:T(8,128)(2,1)S(1)}, u32[]{:S(2)}, u32[]{:S(2)}) collective-permute-start(bf16[16,128]{1,0:T(8,128)(2,1)S(1)} %get-tuple-element.15), channel_id=1, source_target_pairs={{0,385},{1,386},{2,387},{3,388},{4,389},{5,390},{6,391},{7,392},{8... | collective-permute-start | bytes 12296 | tf_op jit(solution)/shard_map/ppermute | solution.py:306
  49.3 1.3 %collective-permute-start.6 = (bf16[16,128]{1,0:T(8,128)(2,1)S(1)}, bf16[16,128]{1,0:T(8,128)(2,1)S(1)}, u32[]{:S(2)}, u32[]{:S(2)}) collective-permute-start(bf16[16,128]{1,0:T(8,128)(2,1)S(1)} %get-tuple-element.16), channel_id=1, source_target_pairs={{128,129},{129,130},{130,131},{131,132},{132,133},{133,134},{134,1... | collective-permute-start | bytes 12296 | tf_op jit(solution)/shard_map/ppermute | solution.py:306

commit v8 on v7

--- a/solution.py
+++ b/solution.py
@@ -77,19 +77,24 @@
     period = CYCLE * PIECE // LANES
     rows[:FLAT, :] = raw[...].astype(jnp.float32).reshape(FLAT, LANES)
     rows[FLAT:, :] = jnp.zeros((rows.shape[0] - FLAT, LANES), jnp.float32)
-    for piece in range(CYCLE):
-        for tile in range(TILES):
-            row, shift = divmod(PIECE * piece + LANES * tile, LANES)
-            value = rows[pl.ds(row, PIECES // CYCLE, stride=period), :]
-            if shift:
-                after = rows[pl.ds(row + 1, PIECES // CYCLE, stride=period), :]
-                value = pltpu.roll(jnp.where(lane >= shift, value, after), LANES - shift, 1)
-            pieces[tile, pl.ds(piece, PIECES // CYCLE, stride=CYCLE), :] = value
-    for tile in range(TILES):
-        ready[:, tile * LANES : (tile + 1) * LANES] = pieces[tile].astype(jnp.bfloat16)
-    copy = pltpu.make_async_copy(ready, out_ref, left)
-    copy.start()
-    copy.wait()
+    copies = []
+    for half in range(2):
+        chosen = range(half * TILES // 2, (half + 1) * TILES // 2)
+        for piece in range(CYCLE):
+            for tile in chosen:
+                row, shift = divmod(PIECE * piece + LANES * tile, LANES)
+                value = rows[pl.ds(row, PIECES // CYCLE, stride=period), :]
+                if shift:
+                    after = rows[pl.ds(row + 1, PIECES // CYCLE, stride=period), :]
+                    value = pltpu.roll(jnp.where(lane >= shift, value, after), LANES - shift, 1)
+                pieces[tile, pl.ds(piece, PIECES // CYCLE, stride=CYCLE), :] = value
+        for tile in chosen:
+            ready[:, tile * LANES : (tile + 1) * LANES] = pieces[tile].astype(jnp.bfloat16)
+        here = pl.ds(half * WIDE // 2, WIDE // 2)
+        copies.append(pltpu.make_async_copy(ready.at[:, here], out_ref.at[:, here], left.at[half]))
+        copies[-1].start()
+    for copy in copies:
+        copy.wait()
 
 
 def body(own_ref, came_ref, t_ref, kern_ref, fwd_ref, inv_ref, first_ref, last_ref, out_ref, xs, near, real, imag, real_back, imag_back, back, ys, flat, sums):
@@ -214,7 +219,7 @@
             pltpu.VMEM((TILES, PIECES, LANES), jnp.float32),
             pltpu.VMEM((PIECES, WIDE), jnp.bfloat16),
             pltpu.SemaphoreType.DMA,
-            pltpu.SemaphoreType.DMA,
+            pltpu.SemaphoreType.DMA((2,)),
         ],
         compiler_params=pltpu.CompilerParams(vmem_limit_bytes=61000 * 1024),
         cost_estimate=pl.CostEstimate(flops=1_000_000, bytes_accessed=800_000, transcendentals=0),

time: 51.5 us -> 51.5 us (level)
  no operation moved by 1% of the time
where the time goes in v8:
time: 51.5 us; the launch traced here: 51.2 us
  starting transfers between devices  32.4 us (63%)
  blocking collectives  10.2 us (20%)
  Pallas kernels  6.63 us (13%)
  waiting for transfers between devices  1.35 us (3%)
    ppermute x6, starting transfers between devices, shards(): arrived.append(lax.ppermute(sent[turn], ('wide', 'blk'), route))  27.9 us
    all_to_all x1, blocking collectives, shards(): lax.all_to_all(partial, 'wide', split_axis=0, concat_axis=0, axis_index_g...  10.2 us
    ppermute x1, starting transfers between devices, from_ahead(): lax.ppermute(block, 'blk', [((i + 1) % count, i) for i in range(count)])  4.47 us
    pallas_call x2, Pallas kernels, gathered(): pl.pallas_call(gather_body, out_shape=jax.ShapeDtypeStruct((PIECES, WIDE)...  3.66 us
    pallas_call x1, Pallas kernels, exchange_term(): pl.pallas_call(body, out_shape=jax.ShapeDtypeStruct((PIECES * TILES, LANE...  2.34 us
  transfers between devices with their start and end apart: 7, of which 2 were waited for; matrix products, arithmetic and copies ran while one was open for 1% of the time, Pallas kernels for 4%

profile of v8, /device:TPU:96, one launch (start us, length us, event | category | flops | bytes accessed | tf_op | source)
XLA Modules:
  0.0 51.2 jit_solution(3139538752029931577)
XLA Ops:
  0.0 1.8 %gather.2.own_ref = bf16[32,2048]{1,0:T(8,128)(2,1)} custom-call(bf16[1,64000]{1,0:T(2,128)(2,1)} %flat_ref.2), custom_call_target="tpu_custom_call" | custom-call | flops 1000000 | bytes 800000 | tf_op jit(solution)/shard_map/gather/pallas_call | solution.py:211
  1.8 4.5 %collective-permute-start = (bf16[32,2048]{1,0:T(8,128)(2,1)}, bf16[32,2048]{1,0:T(8,128)(2,1)S(1)}, u32[]{:S(2)}, u32[]{:S(2)}) collective-permute-start(bf16[32,2048]{1,0:T(8,128)(2,1)} %gather.2.own_ref), channel_id=1, source_target_pairs={{1,0},{2,1},{3,2},{4,3},{5,4},{6,5},{7,6},{8,7},{9,8},{10,9},{11,1... | collective-permute-start | bytes 393224 | tf_op jit(solution)/shard_map/ppermute | solution.py:250
  6.4 0.1 broadcast_add_fusion
  6.4 1.8 %gather.3.t_ref = bf16[32,2048]{1,0:T(8,128)(2,1)} custom-call(bf16[1,64000]{1,0:T(2,128)(2,1)} %flat_ref.3), custom_call_target="tpu_custom_call" | custom-call | flops 1000000 | bytes 800000 | tf_op jit(solution)/shard_map/gather/pallas_call | solution.py:211
  8.3 0.0 copy-start
  8.3 0.0 copy-start.1
  8.3 0.0 copy-start.2
  8.3 0.0 copy-start.3
  8.3 0.0 copy-start.4
  8.3 0.0 copy-start.5
  8.3 0.3 divide_multiply_fusion.kern_ref
  8.6 0.7 %collective-permute-done.came_ref = bf16[32,2048]{1,0:T(8,128)(2,1)S(1)} collective-permute-done((bf16[32,2048]{1,0:T(8,128)(2,1)}, bf16[32,2048]{1,0:T(8,128)(2,1)S(1)}, u32[]{:S(2)}, u32[]{:S(2)}) %collective-permute-start) | collective-permute-done | bytes 131104 | tf_op jit(solution)/shard_map/ppermute | solution.py:250
  9.4 0.0 copy-done
  9.4 0.0 copy-done.1
  9.4 0.0 copy-done.2
  9.4 0.0 copy-done.3
  9.4 0.0 copy-done.4
  9.4 2.3 %exchange.1 = bf16[512,128]{1,0:T(8,128)(2,1)S(1)} custom-call(bf16[32,2048]{1,0:T(8,128)(2,1)S(1)} %copy-done, bf16[32,2048]{1,0:T(8,128)(2,1)S(1)} %collective-permute-done.came_ref, bf16[32,2048]{1,0:T(8,128)(2,1)S(1)} %copy-done.1, f32[40,40,128]{2,1,0:T(8,128)S(1)} %divide_multiply_fusion.kern_ref, bf16[80,80]{1,0:T(8,128)(2,1)S(1)} %copy-done.5, ...), custom_call_target="tpu_custom_call" | custom-call | flops 200000000 | bytes 2000000 | tf_op jit(solution)/shard_map/exchange/pallas_call | solution.py:232
  11.7 10.2 %all_to_all.9.came_ref = bf16[8,64,128]{2,1,0:T(8,128)(2,1)S(1)} all-to-all(bf16[8,64,128]{2,1,0:T(8,128)(2,1)S(1)} %bitcast.3), channel_id=1, replica_groups={{0,16,32,48,64,80,96,112},{128,144,160,176,192,208,224,240},{256,272,28..., dimensions={0} | all-to-all | bytes 262144 | tf_op jit(solution)/shard_map/all_to_all | solution.py:305
  22.0 3.3 %collective-permute-start.1 = (bf16[16,128]{1,0:T(8,128)(2,1)S(1)}, bf16[16,128]{1,0:T(8,128)(2,1)S(1)}, u32[]{:S(2)}, u32[]{:S(2)}) collective-permute-start(bf16[16,128]{1,0:T(8,128)(2,1)S(1)} %get-tuple-element.11), channel_id=1, source_target_pairs={{0,1},{1,2},{2,3},{3,4},{4,5},{5,6},{6,7},{7,8},{8,9},{9,10},{10,1... | collective-permute-start | bytes 12296 | tf_op jit(solution)/shard_map/ppermute | solution.py:311
  25.3 1.3 %collective-permute-start.2 = (bf16[16,128]{1,0:T(8,128)(2,1)S(1)}, bf16[16,128]{1,0:T(8,128)(2,1)S(1)}, u32[]{:S(2)}, u32[]{:S(2)}) collective-permute-start(bf16[16,128]{1,0:T(8,128)(2,1)S(1)} %get-tuple-element.12), channel_id=1, source_target_pairs={{256,1},{257,2},{258,3},{259,4},{260,5},{261,6},{262,7},{263,8},{2... | collective-permute-start | bytes 12296 | tf_op jit(solution)/shard_map/ppermute | solution.py:311
  26.6 7.3 %collective-permute-start.3 = (bf16[16,128]{1,0:T(8,128)(2,1)S(1)}, bf16[16,128]{1,0:T(8,128)(2,1)S(1)}, u32[]{:S(2)}, u32[]{:S(2)}) collective-permute-start(bf16[16,128]{1,0:T(8,128)(2,1)S(1)} %get-tuple-element.13), channel_id=1, source_target_pairs={{0,129},{1,130},{2,131},{3,132},{4,133},{5,134},{6,135},{7,136},{8... | collective-permute-start | bytes 12296 | tf_op jit(solution)/shard_map/ppermute | solution.py:311
  33.9 12.3 %collective-permute-start.4 = (bf16[16,128]{1,0:T(8,128)(2,1)S(1)}, bf16[16,128]{1,0:T(8,128)(2,1)S(1)}, u32[]{:S(2)}, u32[]{:S(2)}) collective-permute-start(bf16[16,128]{1,0:T(8,128)(2,1)S(1)} %get-tuple-element.14), channel_id=1, source_target_pairs={{0,257},{1,258},{2,259},{3,260},{4,261},{5,262},{6,263},{7,264},{8... | collective-permute-start | bytes 12296 | tf_op jit(solution)/shard_map/ppermute | solution.py:311
  46.2 3.1 %collective-permute-start.5 = (bf16[16,128]{1,0:T(8,128)(2,1)S(1)}, bf16[16,128]{1,0:T(8,128)(2,1)S(1)}, u32[]{:S(2)}, u32[]{:S(2)}) collective-permute-start(bf16[16,128]{1,0:T(8,128)(2,1)S(1)} %get-tuple-element.15), channel_id=1, source_target_pairs={{0,385},{1,386},{2,387},{3,388},{4,389},{5,390},{6,391},{7,392},{8... | collective-permute-start | bytes 12296 | tf_op jit(solution)/shard_map/ppermute | solution.py:311
  49.3 0.0 collective-permute-done.1.refs_0_
  49.3 0.7 %collective-permute-start.6 = (bf16[16,128]{1,0:T(8,128)(2,1)S(1)}, bf16[16,128]{1,0:T(8,128)(2,1)S(1)}, u32[]{:S(2)}, u32[]{:S(2)}) collective-permute-start(bf16[16,128]{1,0:T(8,128)(2,1)S(1)} %get-tuple-element.16), channel_id=1, source_target_pairs={{128,129},{129,130},{130,131},{131,132},{132,133},{133,134},{134,1... | collective-permute-start | bytes 12296 | tf_op jit(solution)/shard_map/ppermute | solution.py:311
  50.0 0.0 collective-permute-done.2.refs_1_
  50.0 0.0 collective-permute-done.3.refs_2_
  50.0 0.0 collective-permute-done.4.refs_3_
  50.0 0.6 %collective-permute-done.5.refs_4_ = bf16[16,128]{1,0:T(8,128)(2,1)S(1)} collective-permute-done((bf16[16,128]{1,0:T(8,128)(2,1)S(1)}, bf16[16,128]{1,0:T(8,128)(2,1)S(1)}, u32[]{:S(2)}, u32[]{:S(2)}) %collective-permute-start.5) | collective-permute-done | bytes 4128 | tf_op jit(solution)/shard_map/ppermute | solution.py:311
  50.6 0.0 collective-permute-done.6.refs_5_
  50.6 0.6 %last_sum.1 = f32[16,128]{1,0:T(8,128)} custom-call(bf16[16,128]{1,0:T(8,128)(2,1)S(1)} %collective-permute-done.1.refs_0_, bf16[16,128]{1,0:T(8,128)(2,1)S(1)} %collective-permute-done.2.refs_1_, bf16[16,128]{1,0:T(8,128)(2,1)S(1)} %collective-permute-done.3.refs_2_, bf16[16,128]{1,0:T(8,128)(2,1)S(1)} %collective-permute-done.4.refs_3_, ...), custom_call_target="tpu_custom_call" | custom-call | flops 100000 | bytes 80000 | tf_op jit(solution)/shard_map/last_sum/pallas_call | solution.py:289
  (4 shorter events, 0.1 us)
Async XLA Ops:
  1.8 7.5 %collective-permute-start = (bf16[32,2048]{1,0:T(8,128)(2,1)}, bf16[32,2048]{1,0:T(8,128)(2,1)S(1)}, u32[]{:S(2)}, u32[]{:S(2)}) collective-permute-start(bf16[32,2048]{1,0:T(8,128)(2,1)} %gather.2.own_ref), channel_id=1, source_target_pairs={{1,0},{2,1},{3,2},{4,3},{5,4},{6,5},{7,6},{8,7},{9,8},{10,9},{11,1... | collective-permute-start | bytes 393224 | tf_op jit(solution)/shard_map/ppermute | solution.py:250
  8.3 1.1 %copy-start = (bf16[32,2048]{1,0:T(8,128)(2,1)S(1)}, bf16[32,2048]{1,0:T(8,128)(2,1)}, u32[]{:S(2)}) copy-start(bf16[32,2048]{1,0:T(8,128)(2,1)} %gather.2.own_ref) | copy-start | bytes 393220
  8.3 1.1 %copy-start.1 = (bf16[32,2048]{1,0:T(8,128)(2,1)S(1)}, bf16[32,2048]{1,0:T(8,128)(2,1)}, u32[]{:S(2)}) copy-start(bf16[32,2048]{1,0:T(8,128)(2,1)} %gather.3.t_ref) | copy-start | bytes 393220
  8.3 1.1 %copy-start.2 = (bf16[256,256]{1,0:T(8,128)(2,1)S(1)}, bf16[256,256]{1,0:T(8,128)(2,1)}, u32[]{:S(2)}) copy-start(bf16[256,256]{1,0:T(8,128)(2,1)} %constant.48.clone.last_ref) | copy-start | bytes 393220
  8.3 1.1 %copy-start.3 = (bf16[256,256]{1,0:T(8,128)(2,1)S(1)}, bf16[256,256]{1,0:T(8,128)(2,1)}, u32[]{:S(2)}) copy-start(bf16[256,256]{1,0:T(8,128)(2,1)} %constant.47.clone.first_ref) | copy-start | bytes 393220
  8.3 1.1 %copy-start.4 = (bf16[80,80]{1,0:T(8,128)(2,1)S(1)}, bf16[80,80]{1,0:T(8,128)(2,1)}, u32[]{:S(2)}) copy-start(bf16[80,80]{1,0:T(8,128)(2,1)} %constant.46.clone.inv_ref) | copy-start | bytes 38404
  8.3 1.1 %copy-start.5 = (bf16[80,80]{1,0:T(8,128)(2,1)S(1)}, bf16[80,80]{1,0:T(8,128)(2,1)}, u32[]{:S(2)}) copy-start(bf16[80,80]{1,0:T(8,128)(2,1)} %constant.45.clone.fwd_ref) | copy-start | bytes 38404
  22.0 27.3 %collective-permute-start.1 = (bf16[16,128]{1,0:T(8,128)(2,1)S(1)}, bf16[16,128]{1,0:T(8,128)(2,1)S(1)}, u32[]{:S(2)}, u32[]{:S(2)}) collective-permute-start(bf16[16,128]{1,0:T(8,128)(2,1)S(1)} %get-tuple-element.11), channel_id=1, source_target_pairs={{0,1},{1,2},{2,3},{3,4},{4,5},{5,6},{6,7},{7,8},{8,9},{9,10},{10,1... | collective-permute-start | bytes 12296 | tf_op jit(solution)/shard_map/ppermute | solution.py:311
  25.3 24.7 %collective-permute-start.2 = (bf16[16,128]{1,0:T(8,128)(2,1)S(1)}, bf16[16,128]{1,0:T(8,128)(2,1)S(1)}, u32[]{:S(2)}, u32[]{:S(2)}) collective-permute-start(bf16[16,128]{1,0:T(8,128)(2,1)S(1)} %get-tuple-element.12), channel_id=1, source_target_pairs={{256,1},{257,2},{258,3},{259,4},{260,5},{261,6},{262,7},{263,8},{2... | collective-permute-start | bytes 12296 | tf_op jit(solution)/shard_map/ppermute | solution.py:311
  26.6 23.4 %collective-permute-start.3 = (bf16[16,128]{1,0:T(8,128)(2,1)S(1)}, bf16[16,128]{1,0:T(8,128)(2,1)S(1)}, u32[]{:S(2)}, u32[]{:S(2)}) collective-permute-start(bf16[16,128]{1,0:T(8,128)(2,1)S(1)} %get-tuple-element.13), channel_id=1, source_target_pairs={{0,129},{1,130},{2,131},{3,132},{4,133},{5,134},{6,135},{7,136},{8... | collective-permute-start | bytes 12296 | tf_op jit(solution)/shard_map/ppermute | solution.py:311
  33.9 16.1 %collective-permute-start.4 = (bf16[16,128]{1,0:T(8,128)(2,1)S(1)}, bf16[16,128]{1,0:T(8,128)(2,1)S(1)}, u32[]{:S(2)}, u32[]{:S(2)}) collective-permute-start(bf16[16,128]{1,0:T(8,128)(2,1)S(1)} %get-tuple-element.14), channel_id=1, source_target_pairs={{0,257},{1,258},{2,259},{3,260},{4,261},{5,262},{6,263},{7,264},{8... | collective-permute-start | bytes 12296 | tf_op jit(solution)/shard_map/ppermute | solution.py:311
  46.2 4.4 %collective-permute-start.5 = (bf16[16,128]{1,0:T(8,128)(2,1)S(1)}, bf16[16,128]{1,0:T(8,128)(2,1)S(1)}, u32[]{:S(2)}, u32[]{:S(2)}) collective-permute-start(bf16[16,128]{1,0:T(8,128)(2,1)S(1)} %get-tuple-element.15), channel_id=1, source_target_pairs={{0,385},{1,386},{2,387},{3,388},{4,389},{5,390},{6,391},{7,392},{8... | collective-permute-start | bytes 12296 | tf_op jit(solution)/shard_map/ppermute | solution.py:311
  49.3 1.3 %collective-permute-start.6 = (bf16[16,128]{1,0:T(8,128)(2,1)S(1)}, bf16[16,128]{1,0:T(8,128)(2,1)S(1)}, u32[]{:S(2)}, u32[]{:S(2)}) collective-permute-start(bf16[16,128]{1,0:T(8,128)(2,1)S(1)} %get-tuple-element.16), channel_id=1, source_target_pairs={{128,129},{129,130},{130,131},{131,132},{132,133},{133,134},{134,1... | collective-permute-start | bytes 12296 | tf_op jit(solution)/shard_map/ppermute | solution.py:311
